TPU v7x, 128 devices: a whole 4x4x4 slice. The times are simulated.
128 devices in a mesh: row: 8 (over z_lo, y), col: 16 (over x, z_hi, core).
Axes of the slice: x: 4, y: 4, z: 4 (z_hi: 2, z_lo: 2; z = z_hi * 2 + z_lo), core: 2. Of those that a mesh axis runs over, the one named last changes fastest.
Arguments:
- density: bfloat16 [16, 64, 32768], P('row', None, 'col'), may hold values from -0.8984375 to 0.8984375
- density_rows: int32 [16, 16, 32], replicated, may hold values from 0 to 48, as said below
- square_rows: int32 [16, 16, 32], replicated, may hold values from 0 to 48, as said below
- panel_shift: int32 [16], replicated, may hold values from 0 to 48
Outputs:
- purified: float32 [16, 64, 32768], P('row', None, 'col')
Inputs may be any that keep to these rules, and one draw needn't show every extreme that they name: `density_rows`: for every tile, 32 distinct block rows in increasing order. `square_rows`: for every tile, 32 distinct block rows in increasing order.
All inputs are finite; a program needn't handle non-finite values.
Results may differ from a plain program's by a relative error of at most 0.0029.
Values may be sent and summed in bfloat16 or wider, within the bound.
A program may use at most 64 MiB of HBM per device.

v0:
```python
import jax
import jax.numpy as jnp
from jax import lax
from jax.sharding import PartitionSpec as P

PANEL = 49


def shifted(shard, axis, by):
    devices = lax.axis_size(axis)
    return lax.ppermute(shard, axis, [(i, (i + by) % devices) for i in range(devices)])


def body(density, density_rows, square_rows, panel_shift):
    row_id = lax.axis_index("row")
    col_id = lax.axis_index("col")
    n_col = lax.axis_size("col")
    levels = lax.axis_size("row").bit_length() - 1
    blk = density.shape[1]
    rh = density_rows.shape[2]
    first = 2 * row_id
    own_shift = lax.dynamic_slice(panel_shift, (first,), (2,))

    def make_turn(left_rows, right_rows, out_rows):
        crow = lax.dynamic_slice(out_rows, (first, col_id, 0), (2, 1, rh)).reshape(2, rh)

        def apply_turn(panel, left_tile, right_slot, total):
            arow = lax.dynamic_slice(left_rows, (first, panel, 0), (2, 1, rh)).reshape(2, rh)
            brow = lax.dynamic_slice(right_rows, (panel, col_id, 0), (1, 1, rh)).reshape(rh)
            far_shift = lax.dynamic_slice(panel_shift, (panel,), (1,))
            match_a = arow[:, None, :] == crow[:, :, None]
            has_a = jnp.any(match_a, axis=-1)
            target = jnp.mod(crow + far_shift[0] - own_shift[:, None], PANEL)
            match_b = jnp.logical_and(brow[None, None, :] == target[:, :, None], has_a[:, :, None])
            left_view = left_tile.reshape(2, blk, rh, blk)
            right_view = right_slot.reshape(blk, rh, blk)
            picked_a = jnp.einsum(
                "hea,hxay->hxey",
                match_a.astype(jnp.bfloat16),
                left_view,
                preferred_element_type=jnp.float32,
            ).astype(jnp.bfloat16)
            picked_b = jnp.einsum(
                "heb,xby->hxey",
                match_b.astype(jnp.bfloat16),
                right_view,
                preferred_element_type=jnp.float32,
            ).astype(jnp.bfloat16)
            return total + jnp.einsum(
                "hxey,hyez->hxez", picked_a, picked_b, preferred_element_type=jnp.float32
            )

        return apply_turn

    start = jnp.zeros((2, blk, rh, blk), jnp.float32)

    def align_left(tile):
        for level in range(levels):
            moved = shifted(tile, "col", -(2 ** (level + 1)))
            tile = jnp.where(row_id >> level & 1 == 1, moved, tile)
        return tile

    def align_right(pair):
        moved = jnp.stack([pair[1], shifted(pair[0], "row", -1)])
        pair = jnp.where(col_id & 1 == 1, moved, pair)
        for level in range(1, levels + 1):
            moved = shifted(pair, "row", -(2 ** (level - 1)))
            pair = jnp.where(col_id >> level & 1 == 1, moved, pair)
        return pair

    def multiply(left, left_rows, right, right_rows, out_rows):
        apply_turn = make_turn(left_rows, right_rows, out_rows)

        def round_body(turn_pair, carry):
            left_tile, right_pair, total = carry
            for inner in range(2):
                step = 2 * turn_pair + inner
                panel = (col_id + first + step) % n_col
                total = apply_turn(panel, left_tile, right_pair[0], total)
                left_tile = shifted(left_tile, "col", -1)
                right_pair = jnp.stack([right_pair[1], shifted(right_pair[0], "row", -1)])
            return (left_tile, right_pair, total)

        left_end, right_end, total = lax.fori_loop(0, n_col // 2, round_body, (left, right, start))
        return (total, right_end)

    aligned_right = align_right(density)
    square_total, returned_right = multiply(
        align_left(density), density_rows, aligned_right, density_rows, square_rows
    )
    square = square_total.astype(jnp.bfloat16).reshape(2, blk, rh * blk)
    second_right = align_right(density)
    cube_total, unused_right = multiply(
        align_left(square), square_rows, second_right, density_rows, square_rows
    )
    purified = 3.0 * square.astype(jnp.float32) - 2.0 * cube_total.reshape(2, blk, rh * blk)
    return purified


def solution(mesh):
    placed = (P("row", None, "col"), P(), P(), P())
    return jax.shard_map(
        body, mesh=mesh, in_specs=placed, out_specs=P("row", None, "col"), check_vma=False
    )
```

profile of v0, /device:TPU:1, one launch (start us, length us, event | category | flops | bytes accessed | tf_op | source)
XLA Modules:
  0.0 700.5 jit_solution(17530108641138270047)
XLA Ops:
  0.0 6.6 collective-permute-start.8
  7.7 3.3 collective-permute-start.11
  10.9 6.1 collective-permute-done.11
  18.7 8.8 %collective-permute-start.12 = (bf16[2,64,2048]{2,1,0:T(8,128)(2,1)S(1)}, bf16[2,64,2048]{2,1,0:T(8,128)(2,1)S(1)}, u32[]{:S(2)}, u32[]{:S(2)}) collective-permute-start(bf16[2,64,2048]{2,1,0:T(8,128)(2,1)S(1)} %get-tuple-element.890), channel_id=1, source_target_pairs={{0,112},{16,0},{32,16},{48,32},{64,48},{80,64},{96,80},{112,96},{1... | collective-permute-start | bytes 1572872 | tf_op jit(solution)/shard_map/ppermute | solution.py:11
  28.9 8.3 %collective-permute-done.12 = bf16[2,64,2048]{2,1,0:T(8,128)(2,1)S(1)} collective-permute-done((bf16[2,64,2048]{2,1,0:T(8,128)(2,1)S(1)}, bf16[2,64,2048]{2,1,0:T(8,128)(2,1)S(1)}, u32[]{:S(2)}, u32[]{:S(2)}) %collective-permute-start.12) | collective-permute-done | bytes 524320 | tf_op jit(solution)/shard_map/ppermute | solution.py:11
  41.2 8.6 %collective-permute-done.13 = bf16[2,64,2048]{2,1,0:T(8,128)(2,1)S(1)} collective-permute-done((bf16[2,64,2048]{2,1,0:T(8,128)(2,1)S(1)}, bf16[2,64,2048]{2,1,0:T(8,128)(2,1)S(1)}, u32[]{:S(2)}, u32[]{:S(2)}) %collective-permute-start.13) | collective-permute-done | bytes 524320 | tf_op jit(solution)/shard_map/ppermute | solution.py:11
  53.0 7.1 %collective-permute-done.14 = bf16[2,64,2048]{2,1,0:T(8,128)(2,1)S(1)} collective-permute-done((bf16[2,64,2048]{2,1,0:T(8,128)(2,1)S(1)}, bf16[2,64,2048]{2,1,0:T(8,128)(2,1)S(1)}, u32[]{:S(2)}, u32[]{:S(2)}) %collective-permute-start.14) | collective-permute-done | bytes 524320 | tf_op jit(solution)/shard_map/ppermute | solution.py:11
  62.8 289.6 %while.42 = (s32[]{:T(128)}, bf16[2,64,2048]{2,1,0:T(8,128)(2,1)}, bf16[2,64,2048]{2,1,0:T(8,128)(2,1)}, f32[2,64,32,64]{1,3,2,0:T(8,128)}, s32[]{:T(128)}, /*in...) while((s32[]{:T(128)}, bf16[2,64,2048]{2,1,0:T(8,128)(2,1)}, ...), condition=%wide.region_3.4_spmd.clone, body=%wide.region_0.3_spmd.clone.sunk | while | flops 135287712 | bytes 32511756 | solution.py:84
  62.8 4.3 collective-permute-start
  69.0 5.2 collective-permute-start.2
  89.9 2.8 reshape.200
  97.2 5.9 collective-permute-done.1
  103.1 3.2 collective-permute-start
  125.5 2.8 reshape.200
  128.3 5.8 collective-permute-start.1
  138.7 2.7 collective-permute-start
  160.2 2.8 reshape.200
  163.0 5.9 collective-permute-start.1
  173.4 2.7 collective-permute-start
  196.3 2.8 reshape.200
  199.0 5.8 collective-permute-start.1
  209.5 2.7 collective-permute-start
  231.9 2.8 reshape.200
  234.7 6.1 collective-permute-start.1
  245.1 2.7 collective-permute-start
  267.3 2.8 reshape.200
  270.1 5.8 collective-permute-start.1
  280.5 2.7 collective-permute-start
  303.3 2.8 reshape.200
  306.1 5.8 collective-permute-start.1
  339.3 2.8 reshape.200
  342.0 5.8 collective-permute-start.1
  354.6 7.9 %collective-permute-start.15 = (bf16[2,64,2048]{2,1,0:T(8,128)(2,1)S(1)}, bf16[2,64,2048]{2,1,0:T(8,128)(2,1)S(1)}, u32[]{:S(2)}, u32[]{:S(2)}) collective-permute-start(bf16[2,64,2048]{2,1,0:T(8,128)(2,1)S(1)} %copy.31), channel_id=1, source_target_pairs={{0,14},{1,15},{2,0},{3,1},{4,2},{5,3},{6,4},{7,5},{8,6},{9,7},{10,... | collective-permute-start | bytes 1572872 | tf_op jit(solution)/shard_map/ppermute | solution.py:11
  362.5 9.3 %collective-permute-done.15 = bf16[2,64,2048]{2,1,0:T(8,128)(2,1)S(1)} collective-permute-done((bf16[2,64,2048]{2,1,0:T(8,128)(2,1)S(1)}, bf16[2,64,2048]{2,1,0:T(8,128)(2,1)S(1)}, u32[]{:S(2)}, u32[]{:S(2)}) %collective-permute-start.15) | collective-permute-done | bytes 524320 | tf_op jit(solution)/shard_map/ppermute | solution.py:11
  371.8 2.8 collective-permute-start.16
  374.7 10.1 %collective-permute-done.16 = bf16[2,64,2048]{2,1,0:T(8,128)(2,1)S(1)} collective-permute-done((bf16[2,64,2048]{2,1,0:T(8,128)(2,1)S(1)}, bf16[2,64,2048]{2,1,0:T(8,128)(2,1)S(1)}, u32[]{:S(2)}, u32[]{:S(2)}) %collective-permute-start.16) | collective-permute-done | bytes 524320 | tf_op jit(solution)/shard_map/ppermute | solution.py:11
  384.8 2.8 collective-permute-start.17
  387.6 10.3 %collective-permute-done.17 = bf16[2,64,2048]{2,1,0:T(8,128)(2,1)S(1)} collective-permute-done((bf16[2,64,2048]{2,1,0:T(8,128)(2,1)S(1)}, bf16[2,64,2048]{2,1,0:T(8,128)(2,1)S(1)}, u32[]{:S(2)}, u32[]{:S(2)}) %collective-permute-start.17) | collective-permute-done | bytes 524320 | tf_op jit(solution)/shard_map/ppermute | solution.py:11
  398.8 296.0 %while.43 = (s32[]{:T(128)}, bf16[2,64,2048]{2,1,0:T(8,128)(2,1)}, bf16[2,64,2048]{2,1,0:T(8,128)(2,1)}, f32[2,64,32,64]{1,3,2,0:T(8,128)}, s32[]{:T(128)}, /*in...) while((s32[]{:T(128)}, bf16[2,64,2048]{2,1,0:T(8,128)(2,1)}, ...), condition=%wide.region_7.8_spmd.clone, body=%wide.region_4.7_spmd.clone.sunk | while | flops 135287712 | bytes 32511764 | solution.py:84
  398.8 3.0 collective-permute-start.4
  403.7 4.1 collective-permute-start.6
  424.9 2.8 reshape.204
  427.7 5.9 collective-permute-start.5
  436.2 2.7 collective-permute-done.5
  438.9 2.9 collective-permute-start.4
  461.0 2.8 reshape.204
  463.7 5.8 collective-permute-start.5
  474.2 2.7 collective-permute-start.4
  496.7 2.8 reshape.204
  499.5 5.8 collective-permute-start.5
  534.0 2.8 reshape.204
  536.8 5.8 collective-permute-start.5
  547.2 2.7 collective-permute-start.4
  551.8 4.5 collective-permute-start.6
  573.5 2.8 reshape.204
  576.3 6.1 collective-permute-start.5
  586.7 2.7 collective-permute-start.4
  608.6 2.8 reshape.204
  611.4 6.1 collective-permute-start.5
  621.8 2.7 collective-permute-start.4
  644.3 2.8 reshape.204
  647.1 6.0 collective-permute-start.5
  681.6 2.8 reshape.204
  684.4 6.1 collective-permute-start.5
  (489 shorter events, 413.2 us)
Async XLA Ops:
  0.0 17.5 %collective-permute-start.8 = (bf16[2,64,2048]{2,1,0:T(8,128)(2,1)}, bf16[2,64,2048]{2,1,0:T(8,128)(2,1)S(1)}, u32[]{:S(2)}, u32[]{:S(2)}) collective-permute-start(bf16[2,64,2048]{2,1,0:T(8,128)(2,1)} %param.8), channel_id=1, source_target_pairs={{0,14},{1,15},{2,0},{3,1},{4,2},{5,3},{6,4},{7,5},{8,6},{9,7},{10,... | collective-permute-start | bytes 1572872 | tf_op jit(solution)/shard_map/ppermute | solution.py:11
  18.7 18.5 %collective-permute-start.12 = (bf16[2,64,2048]{2,1,0:T(8,128)(2,1)S(1)}, bf16[2,64,2048]{2,1,0:T(8,128)(2,1)S(1)}, u32[]{:S(2)}, u32[]{:S(2)}) collective-permute-start(bf16[2,64,2048]{2,1,0:T(8,128)(2,1)S(1)} %get-tuple-element.890), channel_id=1, source_target_pairs={{0,112},{16,0},{32,16},{48,32},{64,48},{80,64},{96,80},{112,96},{1... | collective-permute-start | bytes 1572872 | tf_op jit(solution)/shard_map/ppermute | solution.py:11
  27.6 11.9 %collective-permute-start.9 = (bf16[2,64,2048]{2,1,0:T(8,128)(2,1)S(1)}, bf16[2,64,2048]{2,1,0:T(8,128)(2,1)S(1)}, u32[]{:S(2)}, u32[]{:S(2)}) collective-permute-start(bf16[2,64,2048]{2,1,0:T(8,128)(2,1)S(1)} %get-tuple-element.891), channel_id=1, source_target_pairs={{0,12},{1,13},{2,14},{3,15},{4,0},{5,1},{6,2},{7,3},{8,4},{9,5},{1... | collective-permute-start | bytes 1572872 | tf_op jit(solution)/shard_map/ppermute | solution.py:11
  37.2 12.5 %collective-permute-start.13 = (bf16[2,64,2048]{2,1,0:T(8,128)(2,1)S(1)}, bf16[2,64,2048]{2,1,0:T(8,128)(2,1)S(1)}, u32[]{:S(2)}, u32[]{:S(2)}) collective-permute-start(bf16[2,64,2048]{2,1,0:T(8,128)(2,1)S(1)} %broadcast_select_fusion), channel_id=1, source_target_pairs={{0,96},{16,112},{32,0},{48,16},{64,32},{80,48},{96,64},{112,80},{1... | collective-permute-start | bytes 1572872 | tf_op jit(solution)/shard_map/ppermute | solution.py:11
  39.6 12.5 %collective-permute-start.10 = (bf16[2,64,2048]{2,1,0:T(8,128)(2,1)S(1)}, bf16[2,64,2048]{2,1,0:T(8,128)(2,1)S(1)}, u32[]{:S(2)}, u32[]{:S(2)}) collective-permute-start(bf16[2,64,2048]{2,1,0:T(8,128)(2,1)S(1)} %broadcast_select_fusion.6), channel_id=1, source_target_pairs={{0,8},{1,9},{2,10},{3,11},{4,12},{5,13},{6,14},{7,15},{8,0},{9,1},... | collective-permute-start | bytes 1572872 | tf_op jit(solution)/shard_map/ppermute | solution.py:11
  62.8 27.1 %collective-permute-start = (bf16[2,64,2048]{2,1,0:T(8,128)(2,1)}, bf16[2,64,2048]{2,1,0:T(8,128)(2,1)}, u32[]{:S(2)}, u32[]{:S(2)}) collective-permute-start(bf16[2,64,2048]{2,1,0:T(8,128)(2,1)} %get-tuple-element.1120), channel_id=1, source_target_pairs={{0,15},{1,0},{2,1},{3,2},{4,3},{5,4},{6,5},{7,6},{8,7},{9,8},{10,9... | collective-permute-start | bytes 1572872 | tf_op jit(solution)/shard_map/while/body/eval_jaxpr/ppermute | solution.py:11
  69.0 19.0 %collective-permute-start.2 = (bf16[64,2048]{1,0:T(8,128)(2,1)}, bf16[64,2048]{1,0:T(8,128)(2,1)}, u32[]{:S(2)}, u32[]{:S(2)}) collective-permute-start(bf16[64,2048]{1,0:T(8,128)(2,1)} %get-tuple-element.1061), channel_id=1, source_target_pairs={{0,112},{16,0},{32,16},{48,32},{64,48},{80,64},{96,80},{112,96},{1... | collective-permute-start | bytes 786440 | tf_op jit(solution)/shard_map/while/body/eval_jaxpr/ppermute | solution.py:11
  74.2 13.8 %collective-permute-start.3 = (bf16[64,2048]{1,0:T(8,128)(2,1)S(1)}, bf16[64,2048]{1,0:T(8,128)(2,1)}, u32[]{:S(2)}, u32[]{:S(2)}) collective-permute-start(bf16[64,2048]{1,0:T(8,128)(2,1)S(1)} %get-tuple-element.1062), channel_id=1, source_target_pairs={{0,112},{16,0},{32,16},{48,32},{64,48},{80,64},{96,80},{112,96},{1... | collective-permute-start | bytes 786440 | tf_op jit(solution)/shard_map/while/body/eval_jaxpr/ppermute | solution.py:11
  92.7 10.4 %collective-permute-start.1 = (bf16[2,64,2048]{2,1,0:T(8,128)(2,1)}, bf16[2,64,2048]{2,1,0:T(8,128)(2,1)}, u32[]{:S(2)}, u32[]{:S(2)}) collective-permute-start(bf16[2,64,2048]{2,1,0:T(8,128)(2,1)} %collective-permute-done), channel_id=1, source_target_pairs={{0,15},{1,0},{2,1},{3,2},{4,3},{5,4},{6,5},{7,6},{8,7},{9,8},{10,9... | collective-permute-start | bytes 1572872 | tf_op jit(solution)/shard_map/while/body/eval_jaxpr/ppermute | solution.py:11
  103.1 22.4 %collective-permute-start = (bf16[2,64,2048]{2,1,0:T(8,128)(2,1)}, bf16[2,64,2048]{2,1,0:T(8,128)(2,1)}, u32[]{:S(2)}, u32[]{:S(2)}) collective-permute-start(bf16[2,64,2048]{2,1,0:T(8,128)(2,1)} %get-tuple-element.1120), channel_id=1, source_target_pairs={{0,15},{1,0},{2,1},{3,2},{4,3},{5,4},{6,5},{7,6},{8,7},{9,8},{10,9... | collective-permute-start | bytes 1572872 | tf_op jit(solution)/shard_map/while/body/eval_jaxpr/ppermute | solution.py:11
  108.2 15.4 %collective-permute-start.2 = (bf16[64,2048]{1,0:T(8,128)(2,1)}, bf16[64,2048]{1,0:T(8,128)(2,1)}, u32[]{:S(2)}, u32[]{:S(2)}) collective-permute-start(bf16[64,2048]{1,0:T(8,128)(2,1)} %get-tuple-element.1061), channel_id=1, source_target_pairs={{0,112},{16,0},{32,16},{48,32},{64,48},{80,64},{96,80},{112,96},{1... | collective-permute-start | bytes 786440 | tf_op jit(solution)/shard_map/while/body/eval_jaxpr/ppermute | solution.py:11
  109.8 13.7 %collective-permute-start.3 = (bf16[64,2048]{1,0:T(8,128)(2,1)S(1)}, bf16[64,2048]{1,0:T(8,128)(2,1)}, u32[]{:S(2)}, u32[]{:S(2)}) collective-permute-start(bf16[64,2048]{1,0:T(8,128)(2,1)S(1)} %get-tuple-element.1062), channel_id=1, source_target_pairs={{0,112},{16,0},{32,16},{48,32},{64,48},{80,64},{96,80},{112,96},{1... | collective-permute-start | bytes 786440 | tf_op jit(solution)/shard_map/while/body/eval_jaxpr/ppermute | solution.py:11
  138.7 21.5 %collective-permute-start = (bf16[2,64,2048]{2,1,0:T(8,128)(2,1)}, bf16[2,64,2048]{2,1,0:T(8,128)(2,1)}, u32[]{:S(2)}, u32[]{:S(2)}) collective-permute-start(bf16[2,64,2048]{2,1,0:T(8,128)(2,1)} %get-tuple-element.1120), channel_id=1, source_target_pairs={{0,15},{1,0},{2,1},{3,2},{4,3},{5,4},{6,5},{7,6},{8,7},{9,8},{10,9... | collective-permute-start | bytes 1572872 | tf_op jit(solution)/shard_map/while/body/eval_jaxpr/ppermute | solution.py:11
  143.3 15.0 %collective-permute-start.2 = (bf16[64,2048]{1,0:T(8,128)(2,1)}, bf16[64,2048]{1,0:T(8,128)(2,1)}, u32[]{:S(2)}, u32[]{:S(2)}) collective-permute-start(bf16[64,2048]{1,0:T(8,128)(2,1)} %get-tuple-element.1061), channel_id=1, source_target_pairs={{0,112},{16,0},{32,16},{48,32},{64,48},{80,64},{96,80},{112,96},{1... | collective-permute-start | bytes 786440 | tf_op jit(solution)/shard_map/while/body/eval_jaxpr/ppermute | solution.py:11
  144.5 13.7 %collective-permute-start.3 = (bf16[64,2048]{1,0:T(8,128)(2,1)S(1)}, bf16[64,2048]{1,0:T(8,128)(2,1)}, u32[]{:S(2)}, u32[]{:S(2)}) collective-permute-start(bf16[64,2048]{1,0:T(8,128)(2,1)S(1)} %get-tuple-element.1062), channel_id=1, source_target_pairs={{0,112},{16,0},{32,16},{48,32},{64,48},{80,64},{96,80},{112,96},{1... | collective-permute-start | bytes 786440 | tf_op jit(solution)/shard_map/while/body/eval_jaxpr/ppermute | solution.py:11
  163.0 10.4 %collective-permute-start.1 = (bf16[2,64,2048]{2,1,0:T(8,128)(2,1)}, bf16[2,64,2048]{2,1,0:T(8,128)(2,1)}, u32[]{:S(2)}, u32[]{:S(2)}) collective-permute-start(bf16[2,64,2048]{2,1,0:T(8,128)(2,1)} %collective-permute-done), channel_id=1, source_target_pairs={{0,15},{1,0},{2,1},{3,2},{4,3},{5,4},{6,5},{7,6},{8,7},{9,8},{10,9... | collective-permute-start | bytes 1572872 | tf_op jit(solution)/shard_map/while/body/eval_jaxpr/ppermute | solution.py:11
  173.4 22.9 %collective-permute-start = (bf16[2,64,2048]{2,1,0:T(8,128)(2,1)}, bf16[2,64,2048]{2,1,0:T(8,128)(2,1)}, u32[]{:S(2)}, u32[]{:S(2)}) collective-permute-start(bf16[2,64,2048]{2,1,0:T(8,128)(2,1)} %get-tuple-element.1120), channel_id=1, source_target_pairs={{0,15},{1,0},{2,1},{3,2},{4,3},{5,4},{6,5},{7,6},{8,7},{9,8},{10,9... | collective-permute-start | bytes 1572872 | tf_op jit(solution)/shard_map/while/body/eval_jaxpr/ppermute | solution.py:11
  178.0 16.4 %collective-permute-start.2 = (bf16[64,2048]{1,0:T(8,128)(2,1)}, bf16[64,2048]{1,0:T(8,128)(2,1)}, u32[]{:S(2)}, u32[]{:S(2)}) collective-permute-start(bf16[64,2048]{1,0:T(8,128)(2,1)} %get-tuple-element.1061), channel_id=1, source_target_pairs={{0,112},{16,0},{32,16},{48,32},{64,48},{80,64},{96,80},{112,96},{1... | collective-permute-start | bytes 786440 | tf_op jit(solution)/shard_map/while/body/eval_jaxpr/ppermute | solution.py:11
  180.6 13.7 %collective-permute-start.3 = (bf16[64,2048]{1,0:T(8,128)(2,1)S(1)}, bf16[64,2048]{1,0:T(8,128)(2,1)}, u32[]{:S(2)}, u32[]{:S(2)}) collective-permute-start(bf16[64,2048]{1,0:T(8,128)(2,1)S(1)} %get-tuple-element.1062), channel_id=1, source_target_pairs={{0,112},{16,0},{32,16},{48,32},{64,48},{80,64},{96,80},{112,96},{1... | collective-permute-start | bytes 786440 | tf_op jit(solution)/shard_map/while/body/eval_jaxpr/ppermute | solution.py:11
  209.5 22.5 %collective-permute-start = (bf16[2,64,2048]{2,1,0:T(8,128)(2,1)}, bf16[2,64,2048]{2,1,0:T(8,128)(2,1)}, u32[]{:S(2)}, u32[]{:S(2)}) collective-permute-start(bf16[2,64,2048]{2,1,0:T(8,128)(2,1)} %get-tuple-element.1120), channel_id=1, source_target_pairs={{0,15},{1,0},{2,1},{3,2},{4,3},{5,4},{6,5},{7,6},{8,7},{9,8},{10,9... | collective-permute-start | bytes 1572872 | tf_op jit(solution)/shard_map/while/body/eval_jaxpr/ppermute | solution.py:11
  214.1 16.0 %collective-permute-start.2 = (bf16[64,2048]{1,0:T(8,128)(2,1)}, bf16[64,2048]{1,0:T(8,128)(2,1)}, u32[]{:S(2)}, u32[]{:S(2)}) collective-permute-start(bf16[64,2048]{1,0:T(8,128)(2,1)} %get-tuple-element.1061), channel_id=1, source_target_pairs={{0,112},{16,0},{32,16},{48,32},{64,48},{80,64},{96,80},{112,96},{1... | collective-permute-start | bytes 786440 | tf_op jit(solution)/shard_map/while/body/eval_jaxpr/ppermute | solution.py:11
  216.3 13.8 %collective-permute-start.3 = (bf16[64,2048]{1,0:T(8,128)(2,1)S(1)}, bf16[64,2048]{1,0:T(8,128)(2,1)}, u32[]{:S(2)}, u32[]{:S(2)}) collective-permute-start(bf16[64,2048]{1,0:T(8,128)(2,1)S(1)} %get-tuple-element.1062), channel_id=1, source_target_pairs={{0,112},{16,0},{32,16},{48,32},{64,48},{80,64},{96,80},{112,96},{1... | collective-permute-start | bytes 786440 | tf_op jit(solution)/shard_map/while/body/eval_jaxpr/ppermute | solution.py:11
  245.1 22.2 %collective-permute-start = (bf16[2,64,2048]{2,1,0:T(8,128)(2,1)}, bf16[2,64,2048]{2,1,0:T(8,128)(2,1)}, u32[]{:S(2)}, u32[]{:S(2)}) collective-permute-start(bf16[2,64,2048]{2,1,0:T(8,128)(2,1)} %get-tuple-element.1120), channel_id=1, source_target_pairs={{0,15},{1,0},{2,1},{3,2},{4,3},{5,4},{6,5},{7,6},{8,7},{9,8},{10,9... | collective-permute-start | bytes 1572872 | tf_op jit(solution)/shard_map/while/body/eval_jaxpr/ppermute | solution.py:11
  249.7 15.7 %collective-permute-start.2 = (bf16[64,2048]{1,0:T(8,128)(2,1)}, bf16[64,2048]{1,0:T(8,128)(2,1)}, u32[]{:S(2)}, u32[]{:S(2)}) collective-permute-start(bf16[64,2048]{1,0:T(8,128)(2,1)} %get-tuple-element.1061), channel_id=1, source_target_pairs={{0,112},{16,0},{32,16},{48,32},{64,48},{80,64},{96,80},{112,96},{1... | collective-permute-start | bytes 786440 | tf_op jit(solution)/shard_map/while/body/eval_jaxpr/ppermute | solution.py:11
  251.7 13.7 %collective-permute-start.3 = (bf16[64,2048]{1,0:T(8,128)(2,1)S(1)}, bf16[64,2048]{1,0:T(8,128)(2,1)}, u32[]{:S(2)}, u32[]{:S(2)}) collective-permute-start(bf16[64,2048]{1,0:T(8,128)(2,1)S(1)} %get-tuple-element.1062), channel_id=1, source_target_pairs={{0,112},{16,0},{32,16},{48,32},{64,48},{80,64},{96,80},{112,96},{1... | collective-permute-start | bytes 786440 | tf_op jit(solution)/shard_map/while/body/eval_jaxpr/ppermute | solution.py:11
  270.1 10.4 %collective-permute-start.1 = (bf16[2,64,2048]{2,1,0:T(8,128)(2,1)}, bf16[2,64,2048]{2,1,0:T(8,128)(2,1)}, u32[]{:S(2)}, u32[]{:S(2)}) collective-permute-start(bf16[2,64,2048]{2,1,0:T(8,128)(2,1)} %collective-permute-done), channel_id=1, source_target_pairs={{0,15},{1,0},{2,1},{3,2},{4,3},{5,4},{6,5},{7,6},{8,7},{9,8},{10,9... | collective-permute-start | bytes 1572872 | tf_op jit(solution)/shard_map/while/body/eval_jaxpr/ppermute | solution.py:11
  280.5 22.8 %collective-permute-start = (bf16[2,64,2048]{2,1,0:T(8,128)(2,1)}, bf16[2,64,2048]{2,1,0:T(8,128)(2,1)}, u32[]{:S(2)}, u32[]{:S(2)}) collective-permute-start(bf16[2,64,2048]{2,1,0:T(8,128)(2,1)} %get-tuple-element.1120), channel_id=1, source_target_pairs={{0,15},{1,0},{2,1},{3,2},{4,3},{5,4},{6,5},{7,6},{8,7},{9,8},{10,9... | collective-permute-start | bytes 1572872 | tf_op jit(solution)/shard_map/while/body/eval_jaxpr/ppermute | solution.py:11
  285.1 16.3 %collective-permute-start.2 = (bf16[64,2048]{1,0:T(8,128)(2,1)}, bf16[64,2048]{1,0:T(8,128)(2,1)}, u32[]{:S(2)}, u32[]{:S(2)}) collective-permute-start(bf16[64,2048]{1,0:T(8,128)(2,1)} %get-tuple-element.1061), channel_id=1, source_target_pairs={{0,112},{16,0},{32,16},{48,32},{64,48},{80,64},{96,80},{112,96},{1... | collective-permute-start | bytes 786440 | tf_op jit(solution)/shard_map/while/body/eval_jaxpr/ppermute | solution.py:11
  287.6 13.8 %collective-permute-start.3 = (bf16[64,2048]{1,0:T(8,128)(2,1)S(1)}, bf16[64,2048]{1,0:T(8,128)(2,1)}, u32[]{:S(2)}, u32[]{:S(2)}) collective-permute-start(bf16[64,2048]{1,0:T(8,128)(2,1)S(1)} %get-tuple-element.1062), channel_id=1, source_target_pairs={{0,112},{16,0},{32,16},{48,32},{64,48},{80,64},{96,80},{112,96},{1... | collective-permute-start | bytes 786440 | tf_op jit(solution)/shard_map/while/body/eval_jaxpr/ppermute | solution.py:11
  306.1 10.4 %collective-permute-start.1 = (bf16[2,64,2048]{2,1,0:T(8,128)(2,1)}, bf16[2,64,2048]{2,1,0:T(8,128)(2,1)}, u32[]{:S(2)}, u32[]{:S(2)}) collective-permute-start(bf16[2,64,2048]{2,1,0:T(8,128)(2,1)} %collective-permute-done), channel_id=1, source_target_pairs={{0,15},{1,0},{2,1},{3,2},{4,3},{5,4},{6,5},{7,6},{8,7},{9,8},{10,9... | collective-permute-start | bytes 1572872 | tf_op jit(solution)/shard_map/while/body/eval_jaxpr/ppermute | solution.py:11
  316.5 22.7 %collective-permute-start = (bf16[2,64,2048]{2,1,0:T(8,128)(2,1)}, bf16[2,64,2048]{2,1,0:T(8,128)(2,1)}, u32[]{:S(2)}, u32[]{:S(2)}) collective-permute-start(bf16[2,64,2048]{2,1,0:T(8,128)(2,1)} %get-tuple-element.1120), channel_id=1, source_target_pairs={{0,15},{1,0},{2,1},{3,2},{4,3},{5,4},{6,5},{7,6},{8,7},{9,8},{10,9... | collective-permute-start | bytes 1572872 | tf_op jit(solution)/shard_map/while/body/eval_jaxpr/ppermute | solution.py:11
  321.1 16.2 %collective-permute-start.2 = (bf16[64,2048]{1,0:T(8,128)(2,1)}, bf16[64,2048]{1,0:T(8,128)(2,1)}, u32[]{:S(2)}, u32[]{:S(2)}) collective-permute-start(bf16[64,2048]{1,0:T(8,128)(2,1)} %get-tuple-element.1061), channel_id=1, source_target_pairs={{0,112},{16,0},{32,16},{48,32},{64,48},{80,64},{96,80},{112,96},{1... | collective-permute-start | bytes 786440 | tf_op jit(solution)/shard_map/while/body/eval_jaxpr/ppermute | solution.py:11
  323.6 13.8 %collective-permute-start.3 = (bf16[64,2048]{1,0:T(8,128)(2,1)S(1)}, bf16[64,2048]{1,0:T(8,128)(2,1)}, u32[]{:S(2)}, u32[]{:S(2)}) collective-permute-start(bf16[64,2048]{1,0:T(8,128)(2,1)S(1)} %get-tuple-element.1062), channel_id=1, source_target_pairs={{0,112},{16,0},{32,16},{48,32},{64,48},{80,64},{96,80},{112,96},{1... | collective-permute-start | bytes 786440 | tf_op jit(solution)/shard_map/while/body/eval_jaxpr/ppermute | solution.py:11
  342.0 10.4 %collective-permute-start.1 = (bf16[2,64,2048]{2,1,0:T(8,128)(2,1)}, bf16[2,64,2048]{2,1,0:T(8,128)(2,1)}, u32[]{:S(2)}, u32[]{:S(2)}) collective-permute-start(bf16[2,64,2048]{2,1,0:T(8,128)(2,1)} %collective-permute-done), channel_id=1, source_target_pairs={{0,15},{1,0},{2,1},{3,2},{4,3},{5,4},{6,5},{7,6},{8,7},{9,8},{10,9... | collective-permute-start | bytes 1572872 | tf_op jit(solution)/shard_map/while/body/eval_jaxpr/ppermute | solution.py:11
  354.6 17.2 %collective-permute-start.15 = (bf16[2,64,2048]{2,1,0:T(8,128)(2,1)S(1)}, bf16[2,64,2048]{2,1,0:T(8,128)(2,1)S(1)}, u32[]{:S(2)}, u32[]{:S(2)}) collective-permute-start(bf16[2,64,2048]{2,1,0:T(8,128)(2,1)S(1)} %copy.31), channel_id=1, source_target_pairs={{0,14},{1,15},{2,0},{3,1},{4,2},{5,3},{6,4},{7,5},{8,6},{9,7},{10,... | collective-permute-start | bytes 1572872 | tf_op jit(solution)/shard_map/ppermute | solution.py:11
  371.8 12.9 %collective-permute-start.16 = (bf16[2,64,2048]{2,1,0:T(8,128)(2,1)S(1)}, bf16[2,64,2048]{2,1,0:T(8,128)(2,1)S(1)}, u32[]{:S(2)}, u32[]{:S(2)}) collective-permute-start(bf16[2,64,2048]{2,1,0:T(8,128)(2,1)S(1)} %broadcast_select_fusion.3), channel_id=1, source_target_pairs={{0,12},{1,13},{2,14},{3,15},{4,0},{5,1},{6,2},{7,3},{8,4},{9,5},{1... | collective-permute-start | bytes 1572872 | tf_op jit(solution)/shard_map/ppermute | solution.py:11
  384.8 13.1 %collective-permute-start.17 = (bf16[2,64,2048]{2,1,0:T(8,128)(2,1)S(1)}, bf16[2,64,2048]{2,1,0:T(8,128)(2,1)S(1)}, u32[]{:S(2)}, u32[]{:S(2)}) collective-permute-start(bf16[2,64,2048]{2,1,0:T(8,128)(2,1)S(1)} %broadcast_select_fusion.5), channel_id=1, source_target_pairs={{0,8},{1,9},{2,10},{3,11},{4,12},{5,13},{6,14},{7,15},{8,0},{9,1},... | collective-permute-start | bytes 1572872 | tf_op jit(solution)/shard_map/ppermute | solution.py:11
  398.8 26.2 %collective-permute-start.4 = (bf16[2,64,2048]{2,1,0:T(8,128)(2,1)}, bf16[2,64,2048]{2,1,0:T(8,128)(2,1)}, u32[]{:S(2)}, u32[]{:S(2)}) collective-permute-start(bf16[2,64,2048]{2,1,0:T(8,128)(2,1)} %get-tuple-element.1172), channel_id=1, source_target_pairs={{0,15},{1,0},{2,1},{3,2},{4,3},{5,4},{6,5},{7,6},{8,7},{9,8},{10,9... | collective-permute-start | bytes 1572872 | tf_op jit(solution)/shard_map/while/body/eval_jaxpr/ppermute | solution.py:11
  403.7 19.4 %collective-permute-start.6 = (bf16[64,2048]{1,0:T(8,128)(2,1)}, bf16[64,2048]{1,0:T(8,128)(2,1)}, u32[]{:S(2)}, u32[]{:S(2)}) collective-permute-start(bf16[64,2048]{1,0:T(8,128)(2,1)} %get-tuple-element.1088), channel_id=1, source_target_pairs={{0,112},{16,0},{32,16},{48,32},{64,48},{80,64},{96,80},{112,96},{1... | collective-permute-start | bytes 786440 | tf_op jit(solution)/shard_map/while/body/eval_jaxpr/ppermute | solution.py:11
  407.8 15.3 %collective-permute-start.7 = (bf16[64,2048]{1,0:T(8,128)(2,1)S(1)}, bf16[64,2048]{1,0:T(8,128)(2,1)}, u32[]{:S(2)}, u32[]{:S(2)}) collective-permute-start(bf16[64,2048]{1,0:T(8,128)(2,1)S(1)} %get-tuple-element.1089), channel_id=1, source_target_pairs={{0,112},{16,0},{32,16},{48,32},{64,48},{80,64},{96,80},{112,96},{1... | collective-permute-start | bytes 786440 | tf_op jit(solution)/shard_map/while/body/eval_jaxpr/ppermute | solution.py:11
  427.7 11.2 %collective-permute-start.5 = (bf16[2,64,2048]{2,1,0:T(8,128)(2,1)}, bf16[2,64,2048]{2,1,0:T(8,128)(2,1)}, u32[]{:S(2)}, u32[]{:S(2)}) collective-permute-start(bf16[2,64,2048]{2,1,0:T(8,128)(2,1)} %collective-permute-done.4), channel_id=1, source_target_pairs={{0,15},{1,0},{2,1},{3,2},{4,3},{5,4},{6,5},{7,6},{8,7},{9,8},{10,9... | collective-permute-start | bytes 1572872 | tf_op jit(solution)/shard_map/while/body/eval_jaxpr/ppermute | solution.py:11
  438.9 22.0 %collective-permute-start.4 = (bf16[2,64,2048]{2,1,0:T(8,128)(2,1)}, bf16[2,64,2048]{2,1,0:T(8,128)(2,1)}, u32[]{:S(2)}, u32[]{:S(2)}) collective-permute-start(bf16[2,64,2048]{2,1,0:T(8,128)(2,1)} %get-tuple-element.1172), channel_id=1, source_target_pairs={{0,15},{1,0},{2,1},{3,2},{4,3},{5,4},{6,5},{7,6},{8,7},{9,8},{10,9... | collective-permute-start | bytes 1572872 | tf_op jit(solution)/shard_map/while/body/eval_jaxpr/ppermute | solution.py:11
  443.7 15.3 %collective-permute-start.6 = (bf16[64,2048]{1,0:T(8,128)(2,1)}, bf16[64,2048]{1,0:T(8,128)(2,1)}, u32[]{:S(2)}, u32[]{:S(2)}) collective-permute-start(bf16[64,2048]{1,0:T(8,128)(2,1)} %get-tuple-element.1088), channel_id=1, source_target_pairs={{0,112},{16,0},{32,16},{48,32},{64,48},{80,64},{96,80},{112,96},{1... | collective-permute-start | bytes 786440 | tf_op jit(solution)/shard_map/while/body/eval_jaxpr/ppermute | solution.py:11
  443.8 15.3 %collective-permute-start.7 = (bf16[64,2048]{1,0:T(8,128)(2,1)S(1)}, bf16[64,2048]{1,0:T(8,128)(2,1)}, u32[]{:S(2)}, u32[]{:S(2)}) collective-permute-start(bf16[64,2048]{1,0:T(8,128)(2,1)S(1)} %get-tuple-element.1089), channel_id=1, source_target_pairs={{0,112},{16,0},{32,16},{48,32},{64,48},{80,64},{96,80},{112,96},{1... | collective-permute-start | bytes 786440 | tf_op jit(solution)/shard_map/while/body/eval_jaxpr/ppermute | solution.py:11
  474.2 22.5 %collective-permute-start.4 = (bf16[2,64,2048]{2,1,0:T(8,128)(2,1)}, bf16[2,64,2048]{2,1,0:T(8,128)(2,1)}, u32[]{:S(2)}, u32[]{:S(2)}) collective-permute-start(bf16[2,64,2048]{2,1,0:T(8,128)(2,1)} %get-tuple-element.1172), channel_id=1, source_target_pairs={{0,15},{1,0},{2,1},{3,2},{4,3},{5,4},{6,5},{7,6},{8,7},{9,8},{10,9... | collective-permute-start | bytes 1572872 | tf_op jit(solution)/shard_map/while/body/eval_jaxpr/ppermute | solution.py:11
  478.8 16.0 %collective-permute-start.6 = (bf16[64,2048]{1,0:T(8,128)(2,1)}, bf16[64,2048]{1,0:T(8,128)(2,1)}, u32[]{:S(2)}, u32[]{:S(2)}) collective-permute-start(bf16[64,2048]{1,0:T(8,128)(2,1)} %get-tuple-element.1088), channel_id=1, source_target_pairs={{0,112},{16,0},{32,16},{48,32},{64,48},{80,64},{96,80},{112,96},{1... | collective-permute-start | bytes 786440 | tf_op jit(solution)/shard_map/while/body/eval_jaxpr/ppermute | solution.py:11
  479.5 15.3 %collective-permute-start.7 = (bf16[64,2048]{1,0:T(8,128)(2,1)S(1)}, bf16[64,2048]{1,0:T(8,128)(2,1)}, u32[]{:S(2)}, u32[]{:S(2)}) collective-permute-start(bf16[64,2048]{1,0:T(8,128)(2,1)S(1)} %get-tuple-element.1089), channel_id=1, source_target_pairs={{0,112},{16,0},{32,16},{48,32},{64,48},{80,64},{96,80},{112,96},{1... | collective-permute-start | bytes 786440 | tf_op jit(solution)/shard_map/while/body/eval_jaxpr/ppermute | solution.py:11
  499.5 10.4 %collective-permute-start.5 = (bf16[2,64,2048]{2,1,0:T(8,128)(2,1)}, bf16[2,64,2048]{2,1,0:T(8,128)(2,1)}, u32[]{:S(2)}, u32[]{:S(2)}) collective-permute-start(bf16[2,64,2048]{2,1,0:T(8,128)(2,1)} %collective-permute-done.4), channel_id=1, source_target_pairs={{0,15},{1,0},{2,1},{3,2},{4,3},{5,4},{6,5},{7,6},{8,7},{9,8},{10,9... | collective-permute-start | bytes 1572872 | tf_op jit(solution)/shard_map/while/body/eval_jaxpr/ppermute | solution.py:11
  509.9 24.1 %collective-permute-start.4 = (bf16[2,64,2048]{2,1,0:T(8,128)(2,1)}, bf16[2,64,2048]{2,1,0:T(8,128)(2,1)}, u32[]{:S(2)}, u32[]{:S(2)}) collective-permute-start(bf16[2,64,2048]{2,1,0:T(8,128)(2,1)} %get-tuple-element.1172), channel_id=1, source_target_pairs={{0,15},{1,0},{2,1},{3,2},{4,3},{5,4},{6,5},{7,6},{8,7},{9,8},{10,9... | collective-permute-start | bytes 1572872 | tf_op jit(solution)/shard_map/while/body/eval_jaxpr/ppermute | solution.py:11
  514.5 17.6 %collective-permute-start.6 = (bf16[64,2048]{1,0:T(8,128)(2,1)}, bf16[64,2048]{1,0:T(8,128)(2,1)}, u32[]{:S(2)}, u32[]{:S(2)}) collective-permute-start(bf16[64,2048]{1,0:T(8,128)(2,1)} %get-tuple-element.1088), channel_id=1, source_target_pairs={{0,112},{16,0},{32,16},{48,32},{64,48},{80,64},{96,80},{112,96},{1... | collective-permute-start | bytes 786440 | tf_op jit(solution)/shard_map/while/body/eval_jaxpr/ppermute | solution.py:11
  516.8 15.3 %collective-permute-start.7 = (bf16[64,2048]{1,0:T(8,128)(2,1)S(1)}, bf16[64,2048]{1,0:T(8,128)(2,1)}, u32[]{:S(2)}, u32[]{:S(2)}) collective-permute-start(bf16[64,2048]{1,0:T(8,128)(2,1)S(1)} %get-tuple-element.1089), channel_id=1, source_target_pairs={{0,112},{16,0},{32,16},{48,32},{64,48},{80,64},{96,80},{112,96},{1... | collective-permute-start | bytes 786440 | tf_op jit(solution)/shard_map/while/body/eval_jaxpr/ppermute | solution.py:11
  536.8 10.4 %collective-permute-start.5 = (bf16[2,64,2048]{2,1,0:T(8,128)(2,1)}, bf16[2,64,2048]{2,1,0:T(8,128)(2,1)}, u32[]{:S(2)}, u32[]{:S(2)}) collective-permute-start(bf16[2,64,2048]{2,1,0:T(8,128)(2,1)} %collective-permute-done.4), channel_id=1, source_target_pairs={{0,15},{1,0},{2,1},{3,2},{4,3},{5,4},{6,5},{7,6},{8,7},{9,8},{10,9... | collective-permute-start | bytes 1572872 | tf_op jit(solution)/shard_map/while/body/eval_jaxpr/ppermute | solution.py:11
  547.2 26.3 %collective-permute-start.4 = (bf16[2,64,2048]{2,1,0:T(8,128)(2,1)}, bf16[2,64,2048]{2,1,0:T(8,128)(2,1)}, u32[]{:S(2)}, u32[]{:S(2)}) collective-permute-start(bf16[2,64,2048]{2,1,0:T(8,128)(2,1)} %get-tuple-element.1172), channel_id=1, source_target_pairs={{0,15},{1,0},{2,1},{3,2},{4,3},{5,4},{6,5},{7,6},{8,7},{9,8},{10,9... | collective-permute-start | bytes 1572872 | tf_op jit(solution)/shard_map/while/body/eval_jaxpr/ppermute | solution.py:11
  551.8 19.8 %collective-permute-start.6 = (bf16[64,2048]{1,0:T(8,128)(2,1)}, bf16[64,2048]{1,0:T(8,128)(2,1)}, u32[]{:S(2)}, u32[]{:S(2)}) collective-permute-start(bf16[64,2048]{1,0:T(8,128)(2,1)} %get-tuple-element.1088), channel_id=1, source_target_pairs={{0,112},{16,0},{32,16},{48,32},{64,48},{80,64},{96,80},{112,96},{1... | collective-permute-start | bytes 786440 | tf_op jit(solution)/shard_map/while/body/eval_jaxpr/ppermute | solution.py:11
  556.3 15.3 %collective-permute-start.7 = (bf16[64,2048]{1,0:T(8,128)(2,1)S(1)}, bf16[64,2048]{1,0:T(8,128)(2,1)}, u32[]{:S(2)}, u32[]{:S(2)}) collective-permute-start(bf16[64,2048]{1,0:T(8,128)(2,1)S(1)} %get-tuple-element.1089), channel_id=1, source_target_pairs={{0,112},{16,0},{32,16},{48,32},{64,48},{80,64},{96,80},{112,96},{1... | collective-permute-start | bytes 786440 | tf_op jit(solution)/shard_map/while/body/eval_jaxpr/ppermute | solution.py:11
  586.7 21.9 %collective-permute-start.4 = (bf16[2,64,2048]{2,1,0:T(8,128)(2,1)}, bf16[2,64,2048]{2,1,0:T(8,128)(2,1)}, u32[]{:S(2)}, u32[]{:S(2)}) collective-permute-start(bf16[2,64,2048]{2,1,0:T(8,128)(2,1)} %get-tuple-element.1172), channel_id=1, source_target_pairs={{0,15},{1,0},{2,1},{3,2},{4,3},{5,4},{6,5},{7,6},{8,7},{9,8},{10,9... | collective-permute-start | bytes 1572872 | tf_op jit(solution)/shard_map/while/body/eval_jaxpr/ppermute | solution.py:11
  591.3 15.4 %collective-permute-start.6 = (bf16[64,2048]{1,0:T(8,128)(2,1)}, bf16[64,2048]{1,0:T(8,128)(2,1)}, u32[]{:S(2)}, u32[]{:S(2)}) collective-permute-start(bf16[64,2048]{1,0:T(8,128)(2,1)} %get-tuple-element.1088), channel_id=1, source_target_pairs={{0,112},{16,0},{32,16},{48,32},{64,48},{80,64},{96,80},{112,96},{1... | collective-permute-start | bytes 786440 | tf_op jit(solution)/shard_map/while/body/eval_jaxpr/ppermute | solution.py:11
  591.4 15.3 %collective-permute-start.7 = (bf16[64,2048]{1,0:T(8,128)(2,1)S(1)}, bf16[64,2048]{1,0:T(8,128)(2,1)}, u32[]{:S(2)}, u32[]{:S(2)}) collective-permute-start(bf16[64,2048]{1,0:T(8,128)(2,1)S(1)} %get-tuple-element.1089), channel_id=1, source_target_pairs={{0,112},{16,0},{32,16},{48,32},{64,48},{80,64},{96,80},{112,96},{1... | collective-permute-start | bytes 786440 | tf_op jit(solution)/shard_map/while/body/eval_jaxpr/ppermute | solution.py:11
  621.8 22.5 %collective-permute-start.4 = (bf16[2,64,2048]{2,1,0:T(8,128)(2,1)}, bf16[2,64,2048]{2,1,0:T(8,128)(2,1)}, u32[]{:S(2)}, u32[]{:S(2)}) collective-permute-start(bf16[2,64,2048]{2,1,0:T(8,128)(2,1)} %get-tuple-element.1172), channel_id=1, source_target_pairs={{0,15},{1,0},{2,1},{3,2},{4,3},{5,4},{6,5},{7,6},{8,7},{9,8},{10,9... | collective-permute-start | bytes 1572872 | tf_op jit(solution)/shard_map/while/body/eval_jaxpr/ppermute | solution.py:11
  626.4 16.0 %collective-permute-start.6 = (bf16[64,2048]{1,0:T(8,128)(2,1)}, bf16[64,2048]{1,0:T(8,128)(2,1)}, u32[]{:S(2)}, u32[]{:S(2)}) collective-permute-start(bf16[64,2048]{1,0:T(8,128)(2,1)} %get-tuple-element.1088), channel_id=1, source_target_pairs={{0,112},{16,0},{32,16},{48,32},{64,48},{80,64},{96,80},{112,96},{1... | collective-permute-start | bytes 786440 | tf_op jit(solution)/shard_map/while/body/eval_jaxpr/ppermute | solution.py:11
  627.1 15.3 %collective-permute-start.7 = (bf16[64,2048]{1,0:T(8,128)(2,1)S(1)}, bf16[64,2048]{1,0:T(8,128)(2,1)}, u32[]{:S(2)}, u32[]{:S(2)}) collective-permute-start(bf16[64,2048]{1,0:T(8,128)(2,1)S(1)} %get-tuple-element.1089), channel_id=1, source_target_pairs={{0,112},{16,0},{32,16},{48,32},{64,48},{80,64},{96,80},{112,96},{1... | collective-permute-start | bytes 786440 | tf_op jit(solution)/shard_map/while/body/eval_jaxpr/ppermute | solution.py:11
  657.5 24.1 %collective-permute-start.4 = (bf16[2,64,2048]{2,1,0:T(8,128)(2,1)}, bf16[2,64,2048]{2,1,0:T(8,128)(2,1)}, u32[]{:S(2)}, u32[]{:S(2)}) collective-permute-start(bf16[2,64,2048]{2,1,0:T(8,128)(2,1)} %get-tuple-element.1172), channel_id=1, source_target_pairs={{0,15},{1,0},{2,1},{3,2},{4,3},{5,4},{6,5},{7,6},{8,7},{9,8},{10,9... | collective-permute-start | bytes 1572872 | tf_op jit(solution)/shard_map/while/body/eval_jaxpr/ppermute | solution.py:11
  662.1 17.6 %collective-permute-start.6 = (bf16[64,2048]{1,0:T(8,128)(2,1)}, bf16[64,2048]{1,0:T(8,128)(2,1)}, u32[]{:S(2)}, u32[]{:S(2)}) collective-permute-start(bf16[64,2048]{1,0:T(8,128)(2,1)} %get-tuple-element.1088), channel_id=1, source_target_pairs={{0,112},{16,0},{32,16},{48,32},{64,48},{80,64},{96,80},{112,96},{1... | collective-permute-start | bytes 786440 | tf_op jit(solution)/shard_map/while/body/eval_jaxpr/ppermute | solution.py:11
  664.5 15.3 %collective-permute-start.7 = (bf16[64,2048]{1,0:T(8,128)(2,1)S(1)}, bf16[64,2048]{1,0:T(8,128)(2,1)}, u32[]{:S(2)}, u32[]{:S(2)}) collective-permute-start(bf16[64,2048]{1,0:T(8,128)(2,1)S(1)} %get-tuple-element.1089), channel_id=1, source_target_pairs={{0,112},{16,0},{32,16},{48,32},{64,48},{80,64},{96,80},{112,96},{1... | collective-permute-start | bytes 786440 | tf_op jit(solution)/shard_map/while/body/eval_jaxpr/ppermute | solution.py:11
  (48 other events, 400.6 us)
where the time goes:
time: 707 us; the launch traced here: 701 us
  starting transfers between devices  210 us (30%)
  local copies, waits for them, and re-layouts  202 us (29%)
  matrix products  115 us (16%)
  waiting for transfers between devices  97 us (14%)
  other arithmetic  74.6 us (11%)
    ppermute x74, starting transfers between devices, shifted(): lax.ppermute(shard, axis, [(i, (i + by) % devices) for i in range(devices)])  210 us
    ppermute x74, waiting for transfers between devices, shifted(): lax.ppermute(shard, axis, [(i, (i + by) % devices) for i in range(devices)])  97 us
    reshape x32, local copies, waits for them, and re-layouts, apply_turn(): left_view = left_tile.reshape(2, blk, rh, blk)  77.4 us
    dot_general x32, local copies, waits for them, and re-layouts, apply_turn(): jnp.einsum('heb,xby->hxey', match_b.astype(jnp.bfloat16), right_view, pre...  51.1 us
    dot_general x32, matrix products, apply_turn(): jnp.einsum('hea,hxay->hxey', match_a.astype(jnp.bfloat16), left_view, pre...  50.5 us
    dot_general x32, matrix products, apply_turn(): jnp.einsum('hxey,hyez->hxez', picked_a, picked_b, preferred_element_type=...  48.9 us
    select_n x16, other arithmetic, apply_turn(): target = jnp.mod(crow + far_shift[0] - own_shift[:, None], PANEL)  31.1 us
    another operation x16, other arithmetic, round_body(): right_pair = jnp.stack([right_pair[1], shifted(right_pair[0], 'row', -1)])  30.2 us
  transfers between devices with their start and end apart: 74, of which 25 were waited for; matrix products, arithmetic and copies ran while one was open for 48% of the time, Pallas kernels for 0%

commit v1 on v0

v1 whole, which is shorter than its diff:
```python
import jax
import jax.numpy as jnp
from jax import lax
from jax.experimental import pallas as pl
from jax.experimental.pallas import tpu as pltpu
from jax.sharding import PartitionSpec as P

PANEL = 49
BLOCK = 64
SPAN = 2 * BLOCK
RH = 32
NPAN = 16
N_ROW = 8
N_COL = 16
HALF = NPAN * BLOCK // 2
FULL = NPAN * BLOCK
MESH = pl.DeviceIdType.MESH


def home(u):
    last = u // (PANEL - 1)
    x = (u // 12) % 4
    y = (u // 3) % 4
    d = (u % 3 + 1) * (1 - last)
    z = (d + 8 - x - y) % 4
    return (z % 2) * 4 + y, x * 4 + (z // 2) * 2


def low_high(a, b):
    low = jnp.concatenate([a[:, :BLOCK], b[:, :BLOCK]], axis=1)
    high = jnp.concatenate([a[:, BLOCK:], b[:, BLOCK:]], axis=1)
    return low, high


def kernel(
    src_ref, shift_ref, x_ref, srows_ref, out_ref,
    pairs, send, recv, mat, acc, sq, mask, back,
    send_sem, recv_sem, sib_send, sib_recv, back_send, back_recv,
):
    row = lax.axis_index("row")
    col = lax.axis_index("col")
    core = col % 2
    y = row % 4
    z_lo = row // 4
    x = col // 4
    z = 2 * ((col // 2) % 2) + z_lo
    d = (x + y + z) % 4
    corner = (row + col // 2) == 0
    works = jnp.logical_or(d != 0, corner)
    mine = jnp.where(corner, PANEL - 1, (x * 4 + y) * 3 + d - 1)
    own = jnp.logical_and(works, core == z_lo)
    n_own = own.astype(jnp.int32)
    sibling = col + 1 - 2 * core

    barrier = pltpu.get_barrier_semaphore()
    pl.semaphore_signal(barrier, inc=1, device_id=(row, sibling), device_id_type=MESH)

    @pl.when(works)
    def _():
        def greet(s, carry):
            to_row, to_col = 4 * core + s // N_COL, s % N_COL

            @pl.when(jnp.logical_or(to_row != row, to_col != col))
            def _():
                pl.semaphore_signal(barrier, inc=1, device_id=(to_row, to_col), device_id_type=MESH)

            return carry

        lax.fori_loop(0, 4 * N_COL, greet, 0)

    pl.semaphore_wait(barrier, PANEL + 1 - n_own)

    lane = lax.broadcasted_iota(jnp.int32, (1, SPAN), 1)
    left = jnp.where(lane < BLOCK, 1.0, 0.0)
    right = 1.0 - left

    start = (row * N_COL + col) * PANEL // (N_ROW * N_COL)

    for tile in range(2):
        for m in range(RH // 2):
            pairs[tile * (RH // 2) + m] = x_ref[tile, :, m * SPAN : (m + 1) * SPAN]

    def fetch(t, carry):
        u = (start + t) % PANEL
        parts = []
        for tile, side in ((0, left), (1, right)):
            entry = src_ref[tile * PANEL + u]
            has = (entry // RH).astype(jnp.float32)
            e = entry % RH
            wide = pairs[tile * (RH // 2) + e // 2]
            turned = jnp.concatenate([wide[:, BLOCK:], wide[:, :BLOCK]], axis=1)
            picked = jnp.where(e % 2 == tile, wide, turned)
            parts.append(picked * (side * has).astype(jnp.bfloat16))
        send[u] = parts[0] + parts[1]
        to_row, to_first = home(u)
        to_col = to_first + z_lo
        is_self = jnp.logical_and(to_row == row, to_col == col)

        @pl.when(jnp.logical_not(is_self))
        def _():
            pltpu.make_async_remote_copy(
                src_ref=send.at[u],
                dst_ref=recv.at[y, col],
                send_sem=send_sem,
                recv_sem=recv_sem.at[y],
                device_id=(to_row, to_col),
                device_id_type=MESH,
            ).start()

        @pl.when(is_self)
        def _():
            pltpu.make_async_copy(send.at[u], recv.at[y, col], recv_sem.at[y]).start()

        return carry

    lax.fori_loop(0, PANEL, fetch, 0)

    @pl.when(works)
    def _():
        half = pl.multiple_of(core * HALF, HALF)
        there = pl.multiple_of((1 - core) * HALF, HALF)

        spread = jnp.where(
            lax.broadcasted_iota(jnp.int32, (NPAN, FULL), 1) // BLOCK
            == lax.broadcasted_iota(jnp.int32, (NPAN, FULL), 0),
            1.0,
            0.0,
        ).astype(jnp.bfloat16)
        for k in range(NPAN // 2):
            p = core * (NPAN // 2) + k
            past = srows_ref[p] - shift_ref[p]
            hit = jnp.logical_or(past == mine, past == mine - PANEL)
            hit = jnp.where(hit, 1.0, 0.0).astype(jnp.bfloat16)
            count = lax.dot_general(
                jnp.ones((8, RH), jnp.bfloat16), hit, (((1,), (1,)), ((), ())),
                preferred_element_type=jnp.float32,
            ).astype(jnp.bfloat16)
            mask[k] = jnp.dot(count, spread, preferred_element_type=jnp.float32)

        def arrive(g, carry):
            pltpu.make_async_copy(recv.at[g], recv.at[g], recv_sem.at[g]).wait()
            base = pl.multiple_of(core * HALF + g * SPAN, SPAN)
            for c in range(N_COL // 2):
                low, high = low_high(recv[g, 2 * c], recv[g, 2 * c + 1])
                mat[pl.ds(base, BLOCK), pl.ds(c * SPAN, SPAN)] = low
                mat[pl.ds(base + BLOCK, BLOCK), pl.ds(c * SPAN, SPAN)] = high
            pltpu.make_async_remote_copy(
                src_ref=mat.at[pl.ds(base, SPAN)],
                dst_ref=mat.at[pl.ds(base, SPAN)],
                send_sem=sib_send.at[g],
                recv_sem=sib_recv.at[g],
                device_id=(row, sibling),
                device_id_type=MESH,
            ).start()
            return carry

        lax.fori_loop(0, 4, arrive, 0)

        def first(n, carry):
            at = pl.multiple_of(n * 256, 256)
            acc[:, pl.ds(at, 256)] = jnp.dot(
                mat[pl.ds(half, HALF), pl.ds(half, HALF)],
                mat[pl.ds(half, HALF), pl.ds(at, 256)],
                preferred_element_type=jnp.float32,
            )
            return carry

        lax.fori_loop(0, FULL // 256, first, 0)

        def met(g, carry):
            sent = pl.multiple_of(half + g * SPAN, SPAN)
            came = pl.multiple_of(there + g * SPAN, SPAN)
            copy = pltpu.make_async_remote_copy(
                src_ref=mat.at[pl.ds(sent, SPAN)],
                dst_ref=mat.at[pl.ds(came, SPAN)],
                send_sem=sib_send.at[g],
                recv_sem=sib_recv.at[g],
                device_id=(row, sibling),
                device_id_type=MESH,
            )
            copy.wait_send()
            copy.wait_recv()
            return carry

        lax.fori_loop(0, 4, met, 0)

        def second(n, carry):
            at = pl.multiple_of(n * 256, 256)
            more = jnp.dot(
                mat[pl.ds(half, HALF), pl.ds(there, HALF)],
                mat[pl.ds(there, HALF), pl.ds(at, 256)],
                preferred_element_type=jnp.float32,
            )
            whole = acc[:, pl.ds(at, 256)] + more
            for k in range(NPAN // 2):
                keep = mask[k, 0:1, pl.ds(at, 256)]
                sq[k * BLOCK : (k + 1) * BLOCK, pl.ds(at, 256)] = (
                    whole[k * BLOCK : (k + 1) * BLOCK] * keep
                ).astype(jnp.bfloat16)
            return carry

        lax.fori_loop(0, FULL // 256, second, 0)

        def third(n, carry):
            at = pl.multiple_of(n * 256, 256)
            cube = jnp.dot(sq[...], mat[:, pl.ds(at, 256)], preferred_element_type=jnp.float32)
            done = (3.0 * sq[:, pl.ds(at, 256)].astype(jnp.float32) - 2.0 * cube).astype(jnp.bfloat16)
            for g in range(4):
                for c in range(2):
                    top = done[g * SPAN : g * SPAN + BLOCK, c * SPAN : (c + 1) * SPAN]
                    low_part = done[g * SPAN + BLOCK : (g + 1) * SPAN, c * SPAN : (c + 1) * SPAN]
                    low, high = low_high(top, low_part)
                    back[g, 4 * n + 2 * c] = low
                    back[g, 4 * n + 2 * c + 1] = high

            def post(i, inner):
                g, j = i // 4, 4 * n + i % 4
                to_row = 4 * core + g
                is_self = jnp.logical_and(to_row == row, j == col)

                @pl.when(jnp.logical_not(is_self))
                def _():
                    pltpu.make_async_remote_copy(
                        src_ref=back.at[g, j],
                        dst_ref=out_ref.at[mine],
                        send_sem=back_send,
                        recv_sem=back_recv,
                        device_id=(to_row, j),
                        device_id_type=MESH,
                    ).start()

                @pl.when(is_self)
                def _():
                    pltpu.make_async_copy(back.at[g, j], out_ref.at[mine], back_recv).start()

                return inner

            lax.fori_loop(0, 16, post, 0)
            return carry

        lax.fori_loop(0, FULL // 256, third, 0)

    @pl.when(own)
    def _():
        most = send.at[pl.ds(0, PANEL - 1)]
        pltpu.make_async_copy(most, most, send_sem).wait()

    @pl.when(jnp.logical_not(own))
    def _():
        pltpu.make_async_copy(send, send, send_sem).wait()

    @pl.when(own)
    def _():
        flat = back.reshape(4 * N_COL, BLOCK, SPAN).at[pl.ds(0, 4 * N_COL - 1)]
        pltpu.make_async_copy(flat, flat, back_send).wait()

    @pl.when(jnp.logical_and(works, jnp.logical_not(own)))
    def _():
        pltpu.make_async_copy(back, back, back_send).wait()

    pltpu.make_async_copy(out_ref, out_ref, back_recv).wait()


def pick(where_ref, got_ref, out_ref):
    for tile in range(2):
        def two(m, carry, tile=tile):
            a = got_ref[where_ref[tile * RH + 2 * m]].astype(jnp.float32)
            b = got_ref[where_ref[tile * RH + 2 * m + 1]].astype(jnp.float32)
            side = slice(tile * BLOCK, (tile + 1) * BLOCK)
            at = pl.multiple_of(m * SPAN, SPAN)
            out_ref[tile, :, pl.ds(at, SPAN)] = jnp.concatenate([a[:, side], b[:, side]], axis=1)
            return carry

        lax.fori_loop(0, RH // 2, two, 0)


def body(density, density_rows, square_rows, panel_shift):
    row = lax.axis_index("row")
    col = lax.axis_index("col")
    shift = lax.dynamic_slice(panel_shift, (2 * row,), (2,))
    drow = lax.dynamic_slice(density_rows, (2 * row, col, 0), (2, 1, RH)).reshape(2, RH)
    srow = lax.dynamic_slice(square_rows, (2 * row, col, 0), (2, 1, RH)).reshape(2, RH)
    channel = jnp.mod(drow - shift[:, None], PANEL)
    slots = jnp.arange(RH, 2 * RH, dtype=jnp.int32)
    match = channel[:, None, :] == jnp.arange(PANEL, dtype=jnp.int32)[None, :, None]
    source = jnp.sum(jnp.where(match, slots, 0), axis=-1).reshape(-1)
    where = jnp.mod(srow - shift[:, None], PANEL).reshape(-1)

    bf16, f32 = jnp.bfloat16, jnp.float32
    got = pl.pallas_call(
        kernel,
        out_shape=jax.ShapeDtypeStruct((PANEL, BLOCK, SPAN), bf16),
        in_specs=[
            pl.BlockSpec(memory_space=pltpu.SMEM),
            pl.BlockSpec(memory_space=pltpu.SMEM),
            pl.BlockSpec(memory_space=pltpu.VMEM),
            pl.BlockSpec(memory_space=pltpu.VMEM),
        ],
        out_specs=pl.BlockSpec(memory_space=pl.ANY),
        scratch_shapes=[
            pltpu.VMEM((RH, BLOCK, SPAN), bf16),
            pltpu.VMEM((PANEL, BLOCK, SPAN), bf16),
            pltpu.VMEM((4, N_COL, BLOCK, SPAN), bf16),
            pltpu.VMEM((FULL, FULL), bf16),
            pltpu.VMEM((HALF, FULL), f32),
            pltpu.VMEM((HALF, FULL), bf16),
            pltpu.VMEM((NPAN // 2, 8, FULL), f32),
            pltpu.VMEM((4, N_COL, BLOCK, SPAN), bf16),
            pltpu.SemaphoreType.DMA,
            pltpu.SemaphoreType.DMA((4,)),
            pltpu.SemaphoreType.DMA((4,)),
            pltpu.SemaphoreType.DMA((4,)),
            pltpu.SemaphoreType.DMA,
            pltpu.SemaphoreType.DMA,
        ],
        compiler_params=pltpu.CompilerParams(
            collective_id=0, has_side_effects=True, vmem_limit_bytes=40 * 2**20
        ),
    )(source, panel_shift, density, square_rows)
    return pl.pallas_call(
        pick,
        out_shape=jax.ShapeDtypeStruct((2, BLOCK, RH * BLOCK), f32),
        in_specs=[
            pl.BlockSpec(memory_space=pltpu.SMEM),
            pl.BlockSpec(memory_space=pltpu.VMEM),
        ],
        out_specs=pl.BlockSpec(memory_space=pltpu.VMEM),
        compiler_params=pltpu.CompilerParams(vmem_limit_bytes=16 * 2**20),
    )(where, got)


def solution(mesh):
    placed = (P("row", None, "col"), P(), P(), P())
    return jax.shard_map(
        body, mesh=mesh, in_specs=placed, out_specs=P("row", None, "col"), check_vma=False
    )
```

time: 707 us -> 58.4 us (0.08)
  the two profiles are of different devices: /device:TPU:1 before, /device:TPU:31 now
where the time goes in v1:
time: 58.4 us; the launch traced here: 58.2 us
  Pallas kernels  54.2 us (93%)
  local copies, waits for them, and re-layouts  2.99 us (5%)
  other arithmetic  0.91 us (2%)
    pallas_call x1, Pallas kernels, body(): pl.pallas_call(kernel, out_shape=jax.ShapeDtypeStruct((PANEL, BLOCK, SPAN...  50.3 us
    pallas_call x1, Pallas kernels, body(): pl.pallas_call(pick, out_shape=jax.ShapeDtypeStruct((2, BLOCK, RH * BLOCK...  3.92 us
    unnamed x6, local copies, waits for them, and re-layouts  2.6 us

profile of v1, /device:TPU:31, one launch (start us, length us, event | category | flops | bytes accessed | tf_op | source)
XLA Modules:
  0.0 58.2 jit_solution(6154447325738380300)
XLA Ops:
  0.0 0.0 copy-start.2
  0.0 0.7 %copy-done.2 = s32[16]{0:T(128)S(1)} copy-done((s32[16]{0:T(128)S(1)}, s32[16]{0:T(128)}, u32[]{:S(2)}) %copy-start.2) | copy-done | bytes 88
  0.7 0.1 dynamic_slice.10
  0.7 0.1 sub.20
  0.8 0.1 sub.21
  0.9 0.8 %and_select_fusion = (s32[2,1,32]{2,1,0:T(1,128)S(1)}, s32[2,32]{1,0:T(2,128)S(1)}) fusion(s32[16,16,32]{2,1,0:T(8,128)} %param.5, s32[]{:T(128)S(6)} %select_n.26, s32[]{:T(128)S(6)} %select_n.27, s32[2]{0:T(128)S(1)} %dynamic_slice.10, s32[16,16,32]{2,1,0:T(8,128)} %srows_ref.1), kind=kLoop, calls=%fused_computation.2 | loop fusion | flops 448 | bytes 1040 | tf_op jit(solution)/shard_map/jit(remainder)/select_n | solution.py:283
  1.7 0.1 select_reduce_fusion
  1.8 0.1 reshape.16.src_ref
  1.9 0.1 reshape.15
  2.0 0.0 copy-start
  2.0 1.0 %copy-done = bf16[2,64,2048]{2,1,0:T(8,128)(2,1)S(1)} copy-done((bf16[2,64,2048]{2,1,0:T(8,128)(2,1)S(1)}, bf16[2,64,2048]{2,1,0:T(8,128)(2,1)}, u32[]{:S(2)}) %copy-start) | copy-done | bytes 524312
  3.0 0.0 copy-start.1
  3.0 0.9 %copy-done.1 = s32[16,16,32]{2,1,0:T(8,128)S(1)} copy-done((s32[16,16,32]{2,1,0:T(8,128)S(1)}, s32[16,16,32]{2,1,0:T(8,128)}, u32[]{:S(2)}) %copy-start.1) | copy-done | bytes 32792
  3.9 50.3 %shard_map.46.got_ref = bf16[49,64,128]{2,1,0:T(8,128)(2,1)S(1)} custom-call(s32[98]{0:T(128)S(1)} %reshape.16.src_ref, s32[16]{0:T(128)S(1)} %copy-done.2, bf16[2,64,2048]{2,1,0:T(8,128)(2,1)S(1)} %copy-done, s32[16,16,32]{2,1,0:T(8,128)S(1)} %copy-done.1), custom_call_target="tpu_custom_call" | custom-call | tf_op jit(solution)/shard_map/pallas_call | solution.py:290
  54.2 3.9 %shard_map.47 = f32[2,64,2048]{2,1,0:T(8,128)} custom-call(s32[64]{0:T(128)S(1)} %and_select_fusion.1.where_ref, bf16[49,64,128]{2,1,0:T(8,128)(2,1)S(1)} %shard_map.46.got_ref), custom_call_target="tpu_custom_call" | custom-call | tf_op jit(solution)/shard_map/pallas_call | solution.py:320
  (2 shorter events, 0.0 us)
Async XLA Ops:
  0.0 0.7 %copy-start.2 = (s32[16]{0:T(128)S(1)}, s32[16]{0:T(128)}, u32[]{:S(2)}) copy-start(s32[16]{0:T(128)} %shift_ref.1) | copy-start | bytes 196
  2.0 1.0 %copy-start = (bf16[2,64,2048]{2,1,0:T(8,128)(2,1)S(1)}, bf16[2,64,2048]{2,1,0:T(8,128)(2,1)}, u32[]{:S(2)}) copy-start(bf16[2,64,2048]{2,1,0:T(8,128)(2,1)} %x_ref.1) | copy-start | bytes 1572868
  3.0 0.9 %copy-start.1 = (s32[16,16,32]{2,1,0:T(8,128)S(1)}, s32[16,16,32]{2,1,0:T(8,128)}, u32[]{:S(2)}) copy-start(s32[16,16,32]{2,1,0:T(8,128)} %srows_ref.1) | copy-start | bytes 98308

commit v2 on v1

v2 whole, which is shorter than its diff:
```python
import itertools

import jax
import jax.numpy as jnp
from jax import lax
from jax.experimental import pallas as pl
from jax.experimental.pallas import tpu as pltpu
from jax.sharding import PartitionSpec as P

PANEL = 49
BLOCK = 64
SPAN = 2 * BLOCK
RH = 32
NPAN = 16
N_ROW = 8
N_COL = 16
HALF = NPAN * BLOCK // 2
FULL = NPAN * BLOCK
MESH = pl.DeviceIdType.MESH


def wrap(value, size):
    return jnp.where(value >= size, value - size, value)


def order():
    plain = list(itertools.product(range(4), repeat=3))
    return [plain[(i * 27 + 21) % 64] for i in range(64)]


def low_high(a, b):
    low = jnp.concatenate([a[:, :BLOCK], b[:, :BLOCK]], axis=1)
    high = jnp.concatenate([a[:, BLOCK:], b[:, BLOCK:]], axis=1)
    return low, high


def kernel(
    density, drows_hbm, srows_hbm, shift_hbm, out_ref,
    x_ref, drows, srows, shift, blocks, send, recv, mat, acc, sq, mask, back,
    load_sem, send_sem, recv_sem, sib_send, sib_recv, back_send, back_recv, meet_sem,
):
    row = lax.axis_index("row")
    col = lax.axis_index("col")
    core = col % 2
    y = row % 4
    z_lo = row // 4
    x = col // 4
    z_hi = (col // 2) % 2
    z = 2 * z_hi + z_lo
    d = (x + y + z) % 4
    corner = (row + col // 2) == 0
    works = jnp.logical_or(d != 0, corner)
    mine = jnp.where(corner, PANEL - 1, (x * 4 + y) * 3 + d - 1)
    own = jnp.logical_and(works, core == z_lo)
    sibling = col + 1 - 2 * core

    loads = [
        pltpu.make_async_copy(density, x_ref, load_sem.at[0]),
        pltpu.make_async_copy(drows_hbm.at[pl.ds(2 * row, 2)], drows, load_sem.at[1]),
        pltpu.make_async_copy(shift_hbm, shift, load_sem.at[2]),
        pltpu.make_async_copy(srows_hbm.at[pl.ds(core * (NPAN // 2), NPAN // 2)], srows, load_sem.at[3]),
    ]
    for load in loads:
        load.start()

    barrier = pltpu.get_barrier_semaphore()
    for k in range(1, N_COL):
        pl.semaphore_signal(barrier, inc=1, device_id=(row, wrap(col + k, N_COL)), device_id_type=MESH)
    for k in range(1, N_ROW):
        pl.semaphore_signal(barrier, inc=1, device_id=(wrap(row + k, N_ROW), col), device_id_type=MESH)

    loads[0].wait()
    low_side = (lax.broadcasted_iota(jnp.int32, (1, SPAN), 1) < BLOCK).astype(jnp.bfloat16)
    sides = (low_side, 1 - low_side)
    for tile in range(2):
        for m in range(RH // 2):
            wide = x_ref[tile, :, m * SPAN : (m + 1) * SPAN]
            turned = jnp.concatenate([wide[:, BLOCK:], wide[:, :BLOCK]], axis=1)
            first, second = (wide, turned) if tile == 0 else (turned, wide)
            blocks[tile * (RH + 1) + 2 * m] = first * sides[tile]
            blocks[tile * (RH + 1) + 2 * m + 1] = second * sides[tile]
        blocks[tile * (RH + 1) + RH] = jnp.zeros((BLOCK, SPAN), jnp.bfloat16)

    loads[1].wait()
    loads[2].wait()
    loads[3].wait()

    pl.semaphore_wait(barrier, N_COL + N_ROW - 2)
    for k in range(1, N_ROW):
        pl.semaphore_signal(meet_sem, inc=1, device_id=(wrap(row + k, N_ROW), col), device_id_type=MESH)

    begin = []
    for tile in range(2):
        s = shift[2 * row + tile]
        e = jnp.int32(0)
        for i in range(RH):
            e = e + (drows[tile, col, i] < s).astype(jnp.int32)
        begin += [s, wrap(e, RH)]

    def fetch(u, carry):
        r0, e0, r1, e1 = carry
        hit0 = drows[0, col, e0] == r0
        hit1 = drows[1, col, e1] == r1
        send[u] = blocks[jnp.where(hit0, e0, RH)] + blocks[RH + 1 + jnp.where(hit1, e1, RH)]
        e0 = wrap(e0 + hit0.astype(jnp.int32), RH)
        e1 = wrap(e1 + hit1.astype(jnp.int32), RH)
        return wrap(r0 + 1, PANEL), e0, wrap(r1 + 1, PANEL), e1

    lax.fori_loop(0, PANEL, fetch, tuple(begin))

    pl.semaphore_wait(meet_sem, N_ROW - 1)

    xs = [wrap(x + k, 4) for k in range(4)]
    ys = [wrap(y + k, 4) for k in range(4)]

    def post(u, to_x, to_y, to_z, may_stay):
        to_row = (to_z % 2) * 4 + to_y
        to_col = to_x * 4 + (to_z // 2) * 2 + z_lo

        def remote():
            pltpu.make_async_remote_copy(
                src_ref=send.at[u],
                dst_ref=recv.at[y, col],
                send_sem=send_sem,
                recv_sem=recv_sem.at[y],
                device_id=(to_row, to_col),
                device_id_type=MESH,
            ).start()

        def local():
            pltpu.make_async_copy(send.at[u], recv.at[y, col], recv_sem.at[y]).start()

        if may_stay:
            stays = jnp.logical_and(to_row == row, to_col == col)
            pl.when(stays)(local)
            pl.when(jnp.logical_not(stays))(remote)
        else:
            remote()

    zs = [wrap(z + k, 4) for k in range(4)]
    ds = [wrap(d + k, 4) for k in range(4)]
    for dx, dy, dz in order():
        to_x, to_y, to_z, to_d = xs[dx], ys[dy], zs[dz], ds[(dx + dy + dz) % 4]
        u = jnp.where(to_d == 0, PANEL - 1, to_x * 12 + to_y * 3 + to_d - 1)

        @pl.when(jnp.logical_or(to_d != 0, (to_x + to_y + to_z) == 0))
        def _():
            post(u, to_x, to_y, to_z, dx == dy == dz == 0)

    @pl.when(works)
    def _():
        half = pl.multiple_of(core * HALF, HALF)
        there = pl.multiple_of((1 - core) * HALF, HALF)

        spread = jnp.where(
            lax.broadcasted_iota(jnp.int32, (NPAN, FULL), 1) // BLOCK
            == lax.broadcasted_iota(jnp.int32, (NPAN, FULL), 0),
            1.0,
            0.0,
        ).astype(jnp.bfloat16)
        for k in range(NPAN // 2):
            past = srows[k] - shift[core * (NPAN // 2) + k]
            hit = jnp.logical_or(past == mine, past == mine - PANEL)
            hit = jnp.where(hit, 1.0, 0.0).astype(jnp.bfloat16)
            count = lax.dot_general(
                jnp.ones((8, RH), jnp.bfloat16), hit, (((1,), (1,)), ((), ())),
                preferred_element_type=jnp.float32,
            ).astype(jnp.bfloat16)
            mask[k] = jnp.dot(count, spread, preferred_element_type=jnp.float32)

        def arrive(g, carry):
            pltpu.make_async_copy(recv.at[g], recv.at[g], recv_sem.at[g]).wait()
            base = pl.multiple_of(core * HALF + g * SPAN, SPAN)
            for c in range(N_COL // 2):
                low, high = low_high(recv[g, 2 * c], recv[g, 2 * c + 1])
                mat[pl.ds(base, BLOCK), pl.ds(c * SPAN, SPAN)] = low
                mat[pl.ds(base + BLOCK, BLOCK), pl.ds(c * SPAN, SPAN)] = high
            pltpu.make_async_remote_copy(
                src_ref=mat.at[pl.ds(base, SPAN)],
                dst_ref=mat.at[pl.ds(base, SPAN)],
                send_sem=sib_send.at[g],
                recv_sem=sib_recv.at[g],
                device_id=(row, sibling),
                device_id_type=MESH,
            ).start()
            return carry

        lax.fori_loop(0, 4, arrive, 0)

        acc[...] = jnp.dot(
            mat[pl.ds(half, HALF), pl.ds(half, HALF)],
            mat[pl.ds(half, HALF), :],
            preferred_element_type=jnp.float32,
        )

        def met(g, carry):
            sent = pl.multiple_of(half + g * SPAN, SPAN)
            came = pl.multiple_of(there + g * SPAN, SPAN)
            copy = pltpu.make_async_remote_copy(
                src_ref=mat.at[pl.ds(sent, SPAN)],
                dst_ref=mat.at[pl.ds(came, SPAN)],
                send_sem=sib_send.at[g],
                recv_sem=sib_recv.at[g],
                device_id=(row, sibling),
                device_id_type=MESH,
            )
            copy.wait_send()
            copy.wait_recv()
            return carry

        lax.fori_loop(0, 4, met, 0)

        for n in range(FULL // 256):
            at = slice(n * 256, (n + 1) * 256)
            whole = acc[:, at] + jnp.dot(
                mat[pl.ds(half, HALF), pl.ds(there, HALF)],
                mat[pl.ds(there, HALF), at],
                preferred_element_type=jnp.float32,
            )
            for k in range(NPAN // 2):
                part = slice(k * BLOCK, (k + 1) * BLOCK)
                sq[part, at] = (whole[part] * mask[k, 0:1, at]).astype(jnp.bfloat16)

        for i in (2, 1, 3, 0):
            n = xs[i]
            at = pl.multiple_of(n * 256, 256)
            cube = jnp.dot(sq[...], mat[:, pl.ds(at, 256)], preferred_element_type=jnp.float32)
            done = (3.0 * sq[:, pl.ds(at, 256)].astype(jnp.float32) - 2.0 * cube).astype(jnp.bfloat16)
            for g in range(4):
                for c in range(2):
                    top = done[g * SPAN : g * SPAN + BLOCK, c * SPAN : (c + 1) * SPAN]
                    under = done[g * SPAN + BLOCK : (g + 1) * SPAN, c * SPAN : (c + 1) * SPAN]
                    low, high = low_high(top, under)
                    back[g, 4 * n + 2 * c] = low
                    back[g, 4 * n + 2 * c + 1] = high
            for dz, dy, dc in itertools.product((1, 0), (2, 1, 3, 0), range(2)):
                g = ys[dy]
                j = 4 * n + 2 * wrap(z_hi + dz, 2) + wrap(core + dc, 2)
                to_row = 4 * core + g
                remote = jnp.logical_or(to_row != row, j != col)
                if dz == dy == dc == 0:

                    @pl.when(jnp.logical_not(remote))
                    def _():
                        pltpu.make_async_copy(back.at[g, j], out_ref.at[mine], back_recv).start()

                @pl.when(remote)
                def _():
                    pltpu.make_async_remote_copy(
                        src_ref=back.at[g, j],
                        dst_ref=out_ref.at[mine],
                        send_sem=back_send,
                        recv_sem=back_recv,
                        device_id=(to_row, j),
                        device_id_type=MESH,
                    ).start()

    @pl.when(own)
    def _():
        most = send.at[pl.ds(0, PANEL - 1)]
        pltpu.make_async_copy(most, most, send_sem).wait()

    @pl.when(jnp.logical_not(own))
    def _():
        pltpu.make_async_copy(send, send, send_sem).wait()

    @pl.when(own)
    def _():
        flat = back.reshape(4 * N_COL, BLOCK, SPAN).at[pl.ds(0, 4 * N_COL - 1)]
        pltpu.make_async_copy(flat, flat, back_send).wait()

    @pl.when(jnp.logical_and(works, jnp.logical_not(own)))
    def _():
        pltpu.make_async_copy(back, back, back_send).wait()

    pltpu.make_async_copy(out_ref, out_ref, back_recv).wait()


def pick(srows_hbm, shift_hbm, got_hbm, out_hbm, srows, shift, got_ref, out, load_sem, out_sem):
    row = lax.axis_index("row")
    col = lax.axis_index("col")
    loads = [
        pltpu.make_async_copy(srows_hbm.at[pl.ds(2 * row, 2)], srows, load_sem.at[0]),
        pltpu.make_async_copy(shift_hbm, shift, load_sem.at[1]),
        pltpu.make_async_copy(got_hbm, got_ref, load_sem.at[2]),
    ]
    for load in loads:
        load.start()
    for load in loads:
        load.wait()
    parts = []
    for tile in range(2):
        s = shift[2 * row + tile]
        side = slice(tile * BLOCK, (tile + 1) * BLOCK)
        for m in range(RH // 2):
            pair = []
            for e in (2 * m, 2 * m + 1):
                u = srows[tile, col, e] - s
                pair.append(got_ref[jnp.where(u < 0, u + PANEL, u)][:, side])
            out[tile, :, m * SPAN : (m + 1) * SPAN] = jnp.concatenate(pair, axis=1).astype(jnp.float32)
            if m % 4 == 3:
                part = (tile, slice(None), pl.ds((m - 3) * SPAN, 4 * SPAN))
                parts.append(pltpu.make_async_copy(out.at[part], out_hbm.at[part], out_sem.at[len(parts)]))
                parts[-1].start()
    for part in parts:
        part.wait()


def body(density, density_rows, square_rows, panel_shift):
    bf16, f32, i32 = jnp.bfloat16, jnp.float32, jnp.int32
    dma = pltpu.SemaphoreType.DMA
    in_hbm = pl.BlockSpec(memory_space=pltpu.HBM)
    got = pl.pallas_call(
        kernel,
        out_shape=jax.ShapeDtypeStruct((PANEL, BLOCK, SPAN), bf16),
        in_specs=[in_hbm] * 4,
        out_specs=pl.BlockSpec(memory_space=pl.ANY),
        scratch_shapes=[
            pltpu.VMEM((2, BLOCK, RH * BLOCK), bf16),
            pltpu.SMEM((2, N_COL, RH), i32),
            pltpu.VMEM((NPAN // 2, N_COL, RH), i32),
            pltpu.SMEM((NPAN,), i32),
            pltpu.VMEM((2 * (RH + 1), BLOCK, SPAN), bf16),
            pltpu.VMEM((PANEL, BLOCK, SPAN), bf16),
            pltpu.VMEM((4, N_COL, BLOCK, SPAN), bf16),
            pltpu.VMEM((FULL, FULL), bf16),
            pltpu.VMEM((HALF, FULL), f32),
            pltpu.VMEM((HALF, FULL), bf16),
            pltpu.VMEM((NPAN // 2, 8, FULL), f32),
            pltpu.VMEM((4, N_COL, BLOCK, SPAN), bf16),
            dma((4,)),
            dma,
            dma((4,)),
            dma((4,)),
            dma((4,)),
            dma,
            dma,
            pltpu.SemaphoreType.REGULAR,
        ],
        compiler_params=pltpu.CompilerParams(
            collective_id=0, has_side_effects=True, vmem_limit_bytes=60 * 2**20
        ),
    )(density, density_rows, square_rows, panel_shift)
    return pl.pallas_call(
        pick,
        out_shape=jax.ShapeDtypeStruct((2, BLOCK, RH * BLOCK), f32),
        in_specs=[in_hbm] * 3,
        out_specs=pl.BlockSpec(memory_space=pl.ANY),
        scratch_shapes=[
            pltpu.SMEM((2, N_COL, RH), i32),
            pltpu.SMEM((NPAN,), i32),
            pltpu.VMEM((PANEL, BLOCK, SPAN), bf16),
            pltpu.VMEM((2, BLOCK, RH * BLOCK), f32),
            dma((3,)),
            dma((8,)),
        ],
        compiler_params=pltpu.CompilerParams(vmem_limit_bytes=60 * 2**20),
    )(square_rows, panel_shift, got)


def solution(mesh):
    placed = (P("row", None, "col"), P(), P(), P())
    return jax.shard_map(
        body, mesh=mesh, in_specs=placed, out_specs=P("row", None, "col"), check_vma=False
    )
```

time: 58.4 us -> 44.6 us (0.76)
  the two profiles are of different devices: /device:TPU:31 before, /device:TPU:1 now
where the time goes in v2:
time: 44.6 us; the launch traced here: 44.4 us
  Pallas kernels  44.4 us (100%)
    pallas_call x1, Pallas kernels, body(): pl.pallas_call(kernel, out_shape=jax.ShapeDtypeStruct((PANEL, BLOCK, SPAN...  42.1 us
    pallas_call x1, Pallas kernels, body(): pl.pallas_call(pick, out_shape=jax.ShapeDtypeStruct((2, BLOCK, RH * BLOCK...  2.29 us

profile of v2, /device:TPU:1, one launch (start us, length us, event | category | flops | bytes accessed | tf_op | source)
XLA Modules:
  0.0 44.4 jit_solution(13533913106641590469)
XLA Ops:
  0.0 42.1 %shard_map.46.got_hbm = bf16[49,64,128]{2,1,0:T(8,128)(2,1)} custom-call(bf16[2,64,2048]{2,1,0:T(8,128)(2,1)} %density.1, s32[16,16,32]{2,1,0:T(8,128)} %drows_hbm.1, s32[16,16,32]{2,1,0:T(8,128)} %srows_hbm.3, s32[16]{0:T(128)} %shift_hbm.3), custom_call_target="tpu_custom_call" | custom-call | tf_op jit(solution)/shard_map/pallas_call | solution.py:313
  42.2 2.3 %shard_map.47 = f32[2,64,2048]{2,1,0:T(8,128)} custom-call(s32[16,16,32]{2,1,0:T(8,128)} %srows_hbm.3, s32[16]{0:T(128)} %shift_hbm.3, bf16[49,64,128]{2,1,0:T(8,128)(2,1)} %shard_map.46.got_hbm), custom_call_target="tpu_custom_call" | custom-call | tf_op jit(solution)/shard_map/pallas_call | solution.py:344

commit v3 on v2

--- a/solution.py
+++ b/solution.py
@@ -36,7 +36,7 @@
 
 def kernel(
     density, drows_hbm, srows_hbm, shift_hbm, out_ref,
-    x_ref, drows, srows, shift, blocks, send, recv, mat, acc, sq, mask, back,
+    x_ref, drows, srows, kept, shift, got, blocks, send, recv, mat, acc, sq, mask, back,
     load_sem, send_sem, recv_sem, sib_send, sib_recv, back_send, back_recv, meet_sem,
 ):
     row = lax.axis_index("row")
@@ -59,15 +59,31 @@
         pltpu.make_async_copy(drows_hbm.at[pl.ds(2 * row, 2)], drows, load_sem.at[1]),
         pltpu.make_async_copy(shift_hbm, shift, load_sem.at[2]),
         pltpu.make_async_copy(srows_hbm.at[pl.ds(core * (NPAN // 2), NPAN // 2)], srows, load_sem.at[3]),
+        pltpu.make_async_copy(srows_hbm.at[pl.ds(2 * row, 2)], kept, load_sem.at[4]),
     ]
     for load in loads:
         load.start()
 
     barrier = pltpu.get_barrier_semaphore()
-    for k in range(1, N_COL):
-        pl.semaphore_signal(barrier, inc=1, device_id=(row, wrap(col + k, N_COL)), device_id_type=MESH)
-    for k in range(1, N_ROW):
-        pl.semaphore_signal(barrier, inc=1, device_id=(wrap(row + k, N_ROW), col), device_id_type=MESH)
+    pl.semaphore_signal(barrier, inc=1, device_id=(row, sibling), device_id_type=MESH)
+    told = x % 2
+    lone = jnp.logical_and(own, told == core)
+
+    @pl.when(works)
+    def _():
+        chip = col // 2
+        for dy in range(4):
+            to_row = 4 * core + wrap(y + dy, 4)
+            for k in range(N_COL // 2):
+                to_col = 2 * wrap(chip + k, N_COL // 2) + told
+
+                def tell(to_row=to_row, to_col=to_col):
+                    pl.semaphore_signal(barrier, inc=1, device_id=(to_row, to_col), device_id_type=MESH)
+
+                if dy == k == 0:
+                    pl.when(jnp.logical_not(lone))(tell)
+                else:
+                    tell()
 
     loads[0].wait()
     low_side = (lax.broadcasted_iota(jnp.int32, (1, SPAN), 1) < BLOCK).astype(jnp.bfloat16)
@@ -84,10 +100,10 @@
     loads[1].wait()
     loads[2].wait()
     loads[3].wait()
-
-    pl.semaphore_wait(barrier, N_COL + N_ROW - 2)
-    for k in range(1, N_ROW):
-        pl.semaphore_signal(meet_sem, inc=1, device_id=(wrap(row + k, N_ROW), col), device_id_type=MESH)
+    loads[4].wait()
+
+    pl.semaphore_wait(barrier, 1 + PANEL // 2 + (1 - core) - lone.astype(jnp.int32))
+    pl.semaphore_signal(meet_sem, inc=1, device_id=(row, sibling), device_id_type=MESH)
 
     begin = []
     for tile in range(2):
@@ -108,7 +124,7 @@
 
     lax.fori_loop(0, PANEL, fetch, tuple(begin))
 
-    pl.semaphore_wait(meet_sem, N_ROW - 1)
+    pl.semaphore_wait(meet_sem, 1)
 
     xs = [wrap(x + k, 4) for k in range(4)]
     ys = [wrap(y + k, 4) for k in range(4)]
@@ -221,7 +237,33 @@
                 part = slice(k * BLOCK, (k + 1) * BLOCK)
                 sq[part, at] = (whole[part] * mask[k, 0:1, at]).astype(jnp.bfloat16)
 
-        for i in (2, 1, 3, 0):
+        def give(n, to_z, may_stay):
+            for dy, to_core in itertools.product((2, 1, 3, 0), range(2)):
+                g = ys[dy]
+                j = 4 * n + 2 * to_z + to_core
+                to_row = 4 * core + g
+
+                def remote(g=g, j=j, to_row=to_row):
+                    pltpu.make_async_remote_copy(
+                        src_ref=back.at[g, j],
+                        dst_ref=got.at[mine],
+                        send_sem=back_send,
+                        recv_sem=back_recv,
+                        device_id=(to_row, j),
+                        device_id_type=MESH,
+                    ).start()
+
+                def local(g=g, j=j):
+                    pltpu.make_async_copy(back.at[g, j], got.at[mine], back_recv).start()
+
+                if may_stay and dy == 0:
+                    stays = jnp.logical_and(to_row == row, j == col)
+                    pl.when(stays)(local)
+                    pl.when(jnp.logical_not(stays))(remote)
+                else:
+                    remote()
+
+        for k, i in enumerate((2, 1, 3, 0)):
             n = xs[i]
             at = pl.multiple_of(n * 256, 256)
             cube = jnp.dot(sq[...], mat[:, pl.ds(at, 256)], preferred_element_type=jnp.float32)
@@ -233,27 +275,8 @@
                     low, high = low_high(top, under)
                     back[g, 4 * n + 2 * c] = low
                     back[g, 4 * n + 2 * c + 1] = high
-            for dz, dy, dc in itertools.product((1, 0), (2, 1, 3, 0), range(2)):
-                g = ys[dy]
-                j = 4 * n + 2 * wrap(z_hi + dz, 2) + wrap(core + dc, 2)
-                to_row = 4 * core + g
-                remote = jnp.logical_or(to_row != row, j != col)
-                if dz == dy == dc == 0:
-
-                    @pl.when(jnp.logical_not(remote))
-                    def _():
-                        pltpu.make_async_copy(back.at[g, j], out_ref.at[mine], back_recv).start()
-
-                @pl.when(remote)
-                def _():
-                    pltpu.make_async_remote_copy(
-                        src_ref=back.at[g, j],
-                        dst_ref=out_ref.at[mine],
-                        send_sem=back_send,
-                        recv_sem=back_recv,
-                        device_id=(to_row, j),
-                        device_id_type=MESH,
-                    ).start()
+            give(n, 0, i == 0)
+            give(n, 1, i == 0)
 
     @pl.when(own)
     def _():
@@ -273,53 +296,38 @@
     def _():
         pltpu.make_async_copy(back, back, back_send).wait()
 
-    pltpu.make_async_copy(out_ref, out_ref, back_recv).wait()
-
-
-def pick(srows_hbm, shift_hbm, got_hbm, out_hbm, srows, shift, got_ref, out, load_sem, out_sem):
-    row = lax.axis_index("row")
-    col = lax.axis_index("col")
-    loads = [
-        pltpu.make_async_copy(srows_hbm.at[pl.ds(2 * row, 2)], srows, load_sem.at[0]),
-        pltpu.make_async_copy(shift_hbm, shift, load_sem.at[1]),
-        pltpu.make_async_copy(got_hbm, got_ref, load_sem.at[2]),
-    ]
-    for load in loads:
-        load.start()
-    for load in loads:
-        load.wait()
-    parts = []
+    pltpu.make_async_copy(got, got, back_recv).wait()
     for tile in range(2):
         s = shift[2 * row + tile]
         side = slice(tile * BLOCK, (tile + 1) * BLOCK)
         for m in range(RH // 2):
             pair = []
             for e in (2 * m, 2 * m + 1):
-                u = srows[tile, col, e] - s
-                pair.append(got_ref[jnp.where(u < 0, u + PANEL, u)][:, side])
-            out[tile, :, m * SPAN : (m + 1) * SPAN] = jnp.concatenate(pair, axis=1).astype(jnp.float32)
-            if m % 4 == 3:
-                part = (tile, slice(None), pl.ds((m - 3) * SPAN, 4 * SPAN))
-                parts.append(pltpu.make_async_copy(out.at[part], out_hbm.at[part], out_sem.at[len(parts)]))
-                parts[-1].start()
-    for part in parts:
-        part.wait()
+                u = kept[tile, col, e] - s
+                pair.append(got[jnp.where(u < 0, u + PANEL, u)][:, side])
+            out_ref[tile, :, m * SPAN : (m + 1) * SPAN] = jnp.concatenate(pair, axis=1).astype(jnp.float32)
 
 
 def body(density, density_rows, square_rows, panel_shift):
     bf16, f32, i32 = jnp.bfloat16, jnp.float32, jnp.int32
     dma = pltpu.SemaphoreType.DMA
     in_hbm = pl.BlockSpec(memory_space=pltpu.HBM)
-    got = pl.pallas_call(
+    density, density_rows, square_rows, panel_shift = [
+        pltpu.with_memory_space_constraint(v, pltpu.HBM)
+        for v in (density, density_rows, square_rows, panel_shift)
+    ]
+    return pl.pallas_call(
         kernel,
-        out_shape=jax.ShapeDtypeStruct((PANEL, BLOCK, SPAN), bf16),
+        out_shape=jax.ShapeDtypeStruct((2, BLOCK, RH * BLOCK), f32),
         in_specs=[in_hbm] * 4,
-        out_specs=pl.BlockSpec(memory_space=pl.ANY),
+        out_specs=pl.BlockSpec(memory_space=pltpu.VMEM),
         scratch_shapes=[
             pltpu.VMEM((2, BLOCK, RH * BLOCK), bf16),
             pltpu.SMEM((2, N_COL, RH), i32),
             pltpu.VMEM((NPAN // 2, N_COL, RH), i32),
+            pltpu.SMEM((2, N_COL, RH), i32),
             pltpu.SMEM((NPAN,), i32),
+            pltpu.VMEM((PANEL, BLOCK, SPAN), bf16),
             pltpu.VMEM((2 * (RH + 1), BLOCK, SPAN), bf16),
             pltpu.VMEM((PANEL, BLOCK, SPAN), bf16),
             pltpu.VMEM((4, N_COL, BLOCK, SPAN), bf16),
@@ -328,7 +336,7 @@
             pltpu.VMEM((HALF, FULL), bf16),
             pltpu.VMEM((NPAN // 2, 8, FULL), f32),
             pltpu.VMEM((4, N_COL, BLOCK, SPAN), bf16),
-            dma((4,)),
+            dma((5,)),
             dma,
             dma((4,)),
             dma((4,)),
@@ -338,24 +346,9 @@
             pltpu.SemaphoreType.REGULAR,
         ],
         compiler_params=pltpu.CompilerParams(
-            collective_id=0, has_side_effects=True, vmem_limit_bytes=60 * 2**20
+            collective_id=0, has_side_effects=True, vmem_limit_bytes=40 * 2**20
         ),
     )(density, density_rows, square_rows, panel_shift)
-    return pl.pallas_call(
-        pick,
-        out_shape=jax.ShapeDtypeStruct((2, BLOCK, RH * BLOCK), f32),
-        in_specs=[in_hbm] * 3,
-        out_specs=pl.BlockSpec(memory_space=pl.ANY),
-        scratch_shapes=[
-            pltpu.SMEM((2, N_COL, RH), i32),
-            pltpu.SMEM((NPAN,), i32),
-            pltpu.VMEM((PANEL, BLOCK, SPAN), bf16),
-            pltpu.VMEM((2, BLOCK, RH * BLOCK), f32),
-            dma((3,)),
-            dma((8,)),
-        ],
-        compiler_params=pltpu.CompilerParams(vmem_limit_bytes=60 * 2**20),
-    )(square_rows, panel_shift, got)
 
 
 def solution(mesh):

time: 44.6 us -> 43.2 us (0.969)
  Pallas kernels: 44.4 us -> 42.1 us
  local copies, waits for them, and re-layouts: 0 us -> 0.97 us
    pallas_call x2 -> x1, Pallas kernels: 44.4 us -> 42.1 us  [body(): pl.pallas_call(kernel, out_shape=jax.ShapeDtypeStruct((2, BLOCK, RH * BLO...]
    unnamed x0 -> x1, local copies, waits for them, and re-layouts: none -> 0.97 us
where the time goes in v3:
time: 43.2 us; the launch traced here: 43.1 us
  Pallas kernels  42.1 us (97%)
  local copies, waits for them, and re-layouts  0.97 us (2%)
    pallas_call x1, Pallas kernels, body(): pl.pallas_call(kernel, out_shape=jax.ShapeDtypeStruct((2, BLOCK, RH * BLO...  42.1 us
    unnamed x1, local copies, waits for them, and re-layouts  0.97 us

profile of v3, /device:TPU:1, one launch (start us, length us, event | category | flops | bytes accessed | tf_op | source)
XLA Modules:
  0.0 43.1 jit_solution(12368282234597268803)
XLA Ops:
  0.0 42.1 %shard_map.46 = f32[2,64,2048]{2,1,0:T(8,128)S(1)} custom-call(bf16[2,64,2048]{2,1,0:T(8,128)(2,1)} %density.1, s32[16,16,32]{2,1,0:T(8,128)} %drows_hbm.1, s32[16,16,32]{2,1,0:T(8,128)} %srows_hbm.1, s32[16]{0:T(128)} %shift_hbm.1), custom_call_target="tpu_custom_call" | custom-call | tf_op jit(solution)/shard_map/pallas_call | solution.py:319
  42.1 1.0 %copy.6 = f32[2,64,2048]{2,1,0:T(8,128)} copy(f32[2,64,2048]{2,1,0:T(8,128)S(1)} %shard_map.46) | data formatting | bytes 2097152

commit v4 on v3

--- a/solution.py
+++ b/solution.py
@@ -129,22 +129,24 @@
     xs = [wrap(x + k, 4) for k in range(4)]
     ys = [wrap(y + k, 4) for k in range(4)]
 
-    def post(u, to_x, to_y, to_z, may_stay):
+    def post(u, to_x, to_y, to_z, place, may_stay):
+        slot = recv.at[place // 8, place % 8 // 2, core]
+        arrived = recv_sem.at[place // 8]
         to_row = (to_z % 2) * 4 + to_y
         to_col = to_x * 4 + (to_z // 2) * 2 + z_lo
 
         def remote():
             pltpu.make_async_remote_copy(
                 src_ref=send.at[u],
-                dst_ref=recv.at[y, col],
+                dst_ref=slot,
                 send_sem=send_sem,
-                recv_sem=recv_sem.at[y],
+                recv_sem=arrived,
                 device_id=(to_row, to_col),
                 device_id_type=MESH,
             ).start()
 
         def local():
-            pltpu.make_async_copy(send.at[u], recv.at[y, col], recv_sem.at[y]).start()
+            pltpu.make_async_copy(send.at[u], slot, arrived).start()
 
         if may_stay:
             stays = jnp.logical_and(to_row == row, to_col == col)
@@ -155,13 +157,13 @@
 
     zs = [wrap(z + k, 4) for k in range(4)]
     ds = [wrap(d + k, 4) for k in range(4)]
-    for dx, dy, dz in order():
+    for place, (dx, dy, dz) in enumerate(order()):
         to_x, to_y, to_z, to_d = xs[dx], ys[dy], zs[dz], ds[(dx + dy + dz) % 4]
         u = jnp.where(to_d == 0, PANEL - 1, to_x * 12 + to_y * 3 + to_d - 1)
 
         @pl.when(jnp.logical_or(to_d != 0, (to_x + to_y + to_z) == 0))
         def _():
-            post(u, to_x, to_y, to_z, dx == dy == dz == 0)
+            post(u, to_x, to_y, to_z, place, dx == dy == dz == 0)
 
     @pl.when(works)
     def _():
@@ -184,24 +186,28 @@
             ).astype(jnp.bfloat16)
             mask[k] = jnp.dot(count, spread, preferred_element_type=jnp.float32)
 
-        def arrive(g, carry):
-            pltpu.make_async_copy(recv.at[g], recv.at[g], recv_sem.at[g]).wait()
-            base = pl.multiple_of(core * HALF + g * SPAN, SPAN)
-            for c in range(N_COL // 2):
-                low, high = low_high(recv[g, 2 * c], recv[g, 2 * c + 1])
-                mat[pl.ds(base, BLOCK), pl.ds(c * SPAN, SPAN)] = low
-                mat[pl.ds(base + BLOCK, BLOCK), pl.ds(c * SPAN, SPAN)] = high
-            pltpu.make_async_remote_copy(
-                src_ref=mat.at[pl.ds(base, SPAN)],
-                dst_ref=mat.at[pl.ds(base, SPAN)],
-                send_sem=sib_send.at[g],
-                recv_sem=sib_recv.at[g],
-                device_id=(row, sibling),
-                device_id_type=MESH,
-            ).start()
-            return carry
-
-        lax.fori_loop(0, 4, arrive, 0)
+        straight = core == z_lo
+        offsets = order()
+        for k in range(8):
+            pltpu.make_async_copy(recv.at[k], recv.at[k], recv_sem.at[k]).wait()
+            for j in range(4):
+                even, odd = sorted(offsets[8 * k + 2 * j : 8 * k + 2 * j + 2], key=lambda offset: offset[2] % 2)
+                dx, dy, dz = (jnp.where(straight, one, other) for one, other in zip(even, odd))
+                from_x, from_y, from_z = wrap(x + 4 - dx, 4), wrap(y + 4 - dy, 4), wrap(z + 4 - dz, 4)
+                base = pl.multiple_of(core * HALF + from_y * SPAN, SPAN)
+                at = pl.multiple_of((from_x * 2 + from_z // 2) * SPAN, SPAN)
+                low, high = low_high(recv[k, j, 0], recv[k, j, 1])
+                mat[pl.ds(base, BLOCK), pl.ds(at, SPAN)] = low
+                mat[pl.ds(base + BLOCK, BLOCK), pl.ds(at, SPAN)] = high
+                square = mat.at[pl.ds(base, SPAN), pl.ds(at, SPAN)]
+                pltpu.make_async_remote_copy(
+                    src_ref=square,
+                    dst_ref=square,
+                    send_sem=sib_send,
+                    recv_sem=sib_recv,
+                    device_id=(row, sibling),
+                    device_id_type=MESH,
+                ).start()
 
         acc[...] = jnp.dot(
             mat[pl.ds(half, HALF), pl.ds(half, HALF)],
@@ -209,22 +215,8 @@
             preferred_element_type=jnp.float32,
         )
 
-        def met(g, carry):
-            sent = pl.multiple_of(half + g * SPAN, SPAN)
-            came = pl.multiple_of(there + g * SPAN, SPAN)
-            copy = pltpu.make_async_remote_copy(
-                src_ref=mat.at[pl.ds(sent, SPAN)],
-                dst_ref=mat.at[pl.ds(came, SPAN)],
-                send_sem=sib_send.at[g],
-                recv_sem=sib_recv.at[g],
-                device_id=(row, sibling),
-                device_id_type=MESH,
-            )
-            copy.wait_send()
-            copy.wait_recv()
-            return carry
-
-        lax.fori_loop(0, 4, met, 0)
+        came = mat.at[pl.ds(there, HALF)]
+        pltpu.make_async_copy(came, came, sib_recv).wait()
 
         for n in range(FULL // 256):
             at = slice(n * 256, (n + 1) * 256)
@@ -238,7 +230,8 @@
                 sq[part, at] = (whole[part] * mask[k, 0:1, at]).astype(jnp.bfloat16)
 
         def give(n, to_z, may_stay):
-            for dy, to_core in itertools.product((2, 1, 3, 0), range(2)):
+            for dy, dc in itertools.product((2, 1, 3, 0), range(2)):
+                to_core = wrap(core + dc, 2)
                 g = ys[dy]
                 j = 4 * n + 2 * to_z + to_core
                 to_row = 4 * core + g
@@ -275,8 +268,11 @@
                     low, high = low_high(top, under)
                     back[g, 4 * n + 2 * c] = low
                     back[g, 4 * n + 2 * c + 1] = high
-            give(n, 0, i == 0)
-            give(n, 1, i == 0)
+            give(n, 1 - z_hi, i == 0)
+            give(n, z_hi, i == 0)
+
+        went = mat.at[pl.ds(half, HALF)]
+        pltpu.make_async_copy(went, went, sib_send).wait()
 
     @pl.when(own)
     def _():
@@ -330,7 +326,7 @@
             pltpu.VMEM((PANEL, BLOCK, SPAN), bf16),
             pltpu.VMEM((2 * (RH + 1), BLOCK, SPAN), bf16),
             pltpu.VMEM((PANEL, BLOCK, SPAN), bf16),
-            pltpu.VMEM((4, N_COL, BLOCK, SPAN), bf16),
+            pltpu.VMEM((8, 4, 2, BLOCK, SPAN), bf16),
             pltpu.VMEM((FULL, FULL), bf16),
             pltpu.VMEM((HALF, FULL), f32),
             pltpu.VMEM((HALF, FULL), bf16),
@@ -338,9 +334,9 @@
             pltpu.VMEM((4, N_COL, BLOCK, SPAN), bf16),
             dma((5,)),
             dma,
-            dma((4,)),
-            dma((4,)),
-            dma((4,)),
+            dma((8,)),
+            dma,
+            dma,
             dma,
             dma,
             pltpu.SemaphoreType.REGULAR,

time: 43.2 us -> 42.8 us (level)
  no operation moved by 1% of the time
where the time goes in v4:
time: 42.8 us; the launch traced here: 42.7 us
  Pallas kernels  41.7 us (97%)
  local copies, waits for them, and re-layouts  0.97 us (2%)
    pallas_call x1, Pallas kernels, body(): pl.pallas_call(kernel, out_shape=jax.ShapeDtypeStruct((2, BLOCK, RH * BLO...  41.7 us
    unnamed x1, local copies, waits for them, and re-layouts  0.97 us

profile of v4, /device:TPU:1, one launch (start us, length us, event | category | flops | bytes accessed | tf_op | source)
XLA Modules:
  0.0 42.7 jit_solution(17138997395964840109)
XLA Ops:
  0.0 41.7 %shard_map.46 = f32[2,64,2048]{2,1,0:T(8,128)S(1)} custom-call(bf16[2,64,2048]{2,1,0:T(8,128)(2,1)} %density.1, s32[16,16,32]{2,1,0:T(8,128)} %drows_hbm.1, s32[16,16,32]{2,1,0:T(8,128)} %srows_hbm.1, s32[16]{0:T(128)} %shift_hbm.1), custom_call_target="tpu_custom_call" | custom-call | tf_op jit(solution)/shard_map/pallas_call | solution.py:315
  41.7 1.0 %copy.6 = f32[2,64,2048]{2,1,0:T(8,128)} copy(f32[2,64,2048]{2,1,0:T(8,128)S(1)} %shard_map.46) | data formatting | bytes 2097152

commit v5 on v4

--- a/solution.py
+++ b/solution.py
@@ -102,9 +102,6 @@
     loads[3].wait()
     loads[4].wait()
 
-    pl.semaphore_wait(barrier, 1 + PANEL // 2 + (1 - core) - lone.astype(jnp.int32))
-    pl.semaphore_signal(meet_sem, inc=1, device_id=(row, sibling), device_id_type=MESH)
-
     begin = []
     for tile in range(2):
         s = shift[2 * row + tile]
@@ -112,6 +109,9 @@
         for i in range(RH):
             e = e + (drows[tile, col, i] < s).astype(jnp.int32)
         begin += [s, wrap(e, RH)]
+
+    pl.semaphore_wait(barrier, 1 + PANEL // 2 + (1 - core) - lone.astype(jnp.int32))
+    pl.semaphore_signal(meet_sem, inc=1, device_id=(row, sibling), device_id_type=MESH)
 
     def fetch(u, carry):
         r0, e0, r1, e1 = carry
@@ -301,7 +301,7 @@
             for e in (2 * m, 2 * m + 1):
                 u = kept[tile, col, e] - s
                 pair.append(got[jnp.where(u < 0, u + PANEL, u)][:, side])
-            out_ref[tile, :, m * SPAN : (m + 1) * SPAN] = jnp.concatenate(pair, axis=1).astype(jnp.float32)
+            out_ref[tile, :, m * SPAN : (m + 1) * SPAN] = jnp.concatenate(pair, axis=1)
 
 
 def body(density, density_rows, square_rows, panel_shift):
@@ -314,7 +314,7 @@
     ]
     return pl.pallas_call(
         kernel,
-        out_shape=jax.ShapeDtypeStruct((2, BLOCK, RH * BLOCK), f32),
+        out_shape=jax.ShapeDtypeStruct((2, BLOCK, RH * BLOCK), bf16),
         in_specs=[in_hbm] * 4,
         out_specs=pl.BlockSpec(memory_space=pltpu.VMEM),
         scratch_shapes=[
@@ -344,7 +344,7 @@
         compiler_params=pltpu.CompilerParams(
             collective_id=0, has_side_effects=True, vmem_limit_bytes=40 * 2**20
         ),
-    )(density, density_rows, square_rows, panel_shift)
+    )(density, density_rows, square_rows, panel_shift).astype(f32)
 
 
 def solution(mesh):

time: 42.8 us -> 42.9 us (level)
  other arithmetic: 0 us -> 1.08 us
  local copies, waits for them, and re-layouts: 0.97 us -> 0 us
    convert_element_type x0 -> x1, other arithmetic: none -> 1.08 us  [body(): return pl.pallas_call(kernel, out_shape=jax.ShapeDtypeStruct((2, BLOCK, R...]
    unnamed x1 -> x0, local copies, waits for them, and re-layouts: 0.97 us -> none
where the time goes in v5:
time: 42.9 us; the launch traced here: 42.8 us
  Pallas kernels  41.7 us (97%)
  other arithmetic  1.08 us (3%)
    pallas_call x1, Pallas kernels, body(): pl.pallas_call(kernel, out_shape=jax.ShapeDtypeStruct((2, BLOCK, RH * BLO...  41.7 us
    convert_element_type x1, other arithmetic, body(): return pl.pallas_call(kernel, out_shape=jax.ShapeDtypeStruct((2, BLOCK, R...  1.08 us

profile of v5, /device:TPU:1, one launch (start us, length us, event | category | flops | bytes accessed | tf_op | source)
XLA Modules:
  0.0 42.8 jit_solution(15408566099902724827)
XLA Ops:
  0.0 41.7 %shard_map.46 = bf16[2,64,2048]{2,1,0:T(8,128)(2,1)S(1)} custom-call(bf16[2,64,2048]{2,1,0:T(8,128)(2,1)} %density.1, s32[16,16,32]{2,1,0:T(8,128)} %drows_hbm.1, s32[16,16,32]{2,1,0:T(8,128)} %srows_hbm.1, s32[16]{0:T(128)} %shift_hbm.1), custom_call_target="tpu_custom_call" | custom-call | tf_op jit(solution)/shard_map/pallas_call | solution.py:315
  41.7 1.1 %convert_element_type.3 = f32[2,64,2048]{2,1,0:T(8,128)} convert(bf16[2,64,2048]{2,1,0:T(8,128)(2,1)S(1)} %shard_map.46) | non-fusion elementwise | flops 262144 | bytes 1572864 | tf_op jit(solution)/shard_map/convert_element_type | solution.py:347

commit v6 on v4

--- a/solution.py
+++ b/solution.py
@@ -25,7 +25,7 @@
 
 def order():
     plain = list(itertools.product(range(4), repeat=3))
-    return [plain[(i * 27 + 21) % 64] for i in range(64)]
+    return [plain[(i * 19 + 21) % 64] for i in range(64)]
 
 
 def low_high(a, b):
@@ -256,7 +256,7 @@
                 else:
                     remote()
 
-        for k, i in enumerate((2, 1, 3, 0)):
+        for k, i in enumerate((2, 3, 1, 0)):
             n = xs[i]
             at = pl.multiple_of(n * 256, 256)
             cube = jnp.dot(sq[...], mat[:, pl.ds(at, 256)], preferred_element_type=jnp.float32)

time: 42.8 us -> 42.7 us (level)
  no operation moved by 1% of the time
where the time goes in v6:
time: 42.7 us; the launch traced here: 42.4 us
  Pallas kernels  41.4 us (97%)
  local copies, waits for them, and re-layouts  0.97 us (2%)
    pallas_call x1, Pallas kernels, body(): pl.pallas_call(kernel, out_shape=jax.ShapeDtypeStruct((2, BLOCK, RH * BLO...  41.4 us
    unnamed x1, local copies, waits for them, and re-layouts  0.97 us

profile of v6, /device:TPU:1, one launch (start us, length us, event | category | flops | bytes accessed | tf_op | source)
XLA Modules:
  0.0 42.4 jit_solution(10992783907673899928)
XLA Ops:
  0.0 41.4 %shard_map.46 = f32[2,64,2048]{2,1,0:T(8,128)S(1)} custom-call(bf16[2,64,2048]{2,1,0:T(8,128)(2,1)} %density.1, s32[16,16,32]{2,1,0:T(8,128)} %drows_hbm.1, s32[16,16,32]{2,1,0:T(8,128)} %srows_hbm.1, s32[16]{0:T(128)} %shift_hbm.1), custom_call_target="tpu_custom_call" | custom-call | tf_op jit(solution)/shard_map/pallas_call | solution.py:315
  41.5 1.0 %copy.6 = f32[2,64,2048]{2,1,0:T(8,128)} copy(f32[2,64,2048]{2,1,0:T(8,128)S(1)} %shard_map.46) | data formatting | bytes 2097152
